TPU v7x, 512 devices: a whole 4x8x8 slice. The times are simulated.
512 devices in a mesh: ens: 16 (over x, y_lo), lat: 32 (over y_hi, z, core).
Axes of the slice: x: 4, y: 8 (y_hi: 2, y_lo: 4; y = y_hi * 4 + y_lo), z: 8, core: 2. Of those that a mesh axis runs over, the one named last changes fastest.
Arguments:
- features: bfloat16 [128, 128, 128], P('lat'), may hold values from -6 to 6
- random_perturbation: bfloat16 [16, 128, 128, 128], P('ens', 'lat'), may hold values from -6 to 6
- observed_truth: float32 [69, 128, 128], P(None, 'lat'), may hold values from -6 to 6
- stencil_taps: float32 [49, 128], replicated, may hold values from -0.875 to 0.875
- affine_factor: float32 [128], replicated, may hold values from 0.5 to 1.5
- widen_matrix: bfloat16 [512, 128], P('lat'), may hold values from -0.5 to 0.5
- shrink_matrix: bfloat16 [512, 128], P('lat'), may hold values from -0.25 to 0.25
- readout_matrix: bfloat16 [69, 128], replicated, may hold values from -0.5 to 0.5
Outputs:
- crps_score: float32 [], replicated
- stencil_taps_sensitivity: float32 [49, 128], replicated
- affine_factor_sensitivity: float32 [128], replicated
- widen_matrix_sensitivity: float32 [512, 128], P('lat')
- shrink_matrix_sensitivity: float32 [512, 128], P('lat')
- readout_matrix_sensitivity: float32 [69, 128], replicated
- sample_outlook: bfloat16 [16, 69, 128, 128], P('ens', None, 'lat')
- sample_average_spread: float32 [16, 69, 128, 128], P('ens', None, 'lat')
All inputs are finite; a program needn't handle non-finite values.
Results may differ from a plain program's by a relative error of at most 0.0024.
The roundings to bfloat16 on the way count: a program that leaves them out, or rounds other values in their place, can miss the bound.
Values may be sent and summed in bfloat16 or wider, within the bound.
No kernel may reach another device: no remote copies, remote signals or barrier semaphores. Data moves between devices by JAX's collectives and lax.ppermute only.
A program may use at most 64 MiB of HBM per device.

v0:
```python
import math

import jax
import jax.numpy as jnp
from jax import lax
from jax.experimental import pallas as pl
from jax.experimental.pallas import tpu as pltpu
from jax.sharding import PartitionSpec as P

STENCIL_SIDE = 7
SQRT_TWO_PI = 0.7978845608028654
CUBIC = 0.044715
EPSILON = 1e-06
SMOOTHING = 0.01
PER_CHUNK = 5
CHUNK_ROWS = 8
EDGE = 8
STRIP = 16
TAPS_AT = 69
DEPTH_Z = 8
F32, BF16 = jnp.float32, jnp.bfloat16


def core_swap(value):
    count = lax.axis_size("lat")
    return lax.ppermute(value, "lat", [(i, i ^ 1) for i in range(count)])


def odd_swap(value):
    count = lax.axis_size("lat")
    pairs = [(i, i + 1) for i in range(1, count - 1, 2)]
    return lax.ppermute(value, "lat", pairs + [(b, a) for a, b in pairs])


def halo_rows(field, half):
    even = lax.rem(lax.axis_index("lat"), 2) == 0
    head, tail = field[:half], field[field.shape[0] - half :]
    return core_swap(jnp.where(even, tail, head)), odd_swap(jnp.where(even, head, tail))


def exchange(value, axis, groups=None):
    return lax.all_to_all(value, axis, 0, 0, tiled=True, axis_index_groups=groups)


AXES = ("ens", "lat")


def weight_groups(members, bands):
    half = bands // 2
    groups = []
    for e in range(members):
        far = e // 4 * 4 + (e + 2) % 4
        for c in range(2):
            groups.append(
                [e * bands + b for b in range(c, half, 2)]
                + [far * bands + b for b in range(half + c, bands, 2)]
            )
    return groups


def plane_groups(members, bands):
    half = bands // 2
    return [
        [e * bands + h * half + rest for e in range(members) for h in range(2)]
        for rest in range(half)
    ]


def gelu_value(u):
    inner = jnp.tanh(SQRT_TWO_PI * (u + CUBIC * u * u * u))
    return 0.5 * u * (1.0 + inner)


def gelu_slope(u):
    inner = jnp.tanh(SQRT_TWO_PI * (u + CUBIC * u * u * u))
    return 0.5 * (1.0 + inner) + 0.5 * u * (1.0 - inner * inner) * SQRT_TWO_PI * (
        1.0 + 3.0 * CUBIC * u * u
    )


def vmem_call(body, outs, scratch=(), scalars=0, vectors=0, kept=(), aliases=None):
    vmem = pl.BlockSpec(memory_space=pltpu.VMEM)
    smem = pl.BlockSpec(memory_space=pltpu.SMEM)
    call = pl.pallas_call(
        body,
        out_shape=[
            jax.ShapeDtypeStruct(*out) if i in kept else pltpu.VMEM(*out)
            for i, out in enumerate(outs)
        ],
        in_specs=[smem] * scalars + [vmem] * vectors,
        out_specs=[vmem] * len(outs),
        scratch_shapes=list(scratch),
        input_output_aliases=aliases or {},
        compiler_params=pltpu.CompilerParams(vmem_limit_bytes=16 << 20),
    )

    def run(*operands):
        operands = operands[:scalars] + tuple(
            pltpu.with_memory_space_constraint(x, pltpu.VMEM) for x in operands[scalars:]
        )
        return call(*operands)

    return run


def dot(a, b, contract):
    return lax.dot_general(a, b, ((contract[:1], contract[1:]), ((), ())), preferred_element_type=F32)


def stencil_body(place, field, partner, other, taps, gain, ext, scaled, inverse, normed):
    even = place[0] == 0
    rows, zonal, _ = field.shape
    half = STENCIL_SIDE // 2
    for r in range(rows + 2 * half):
        if r < half:
            row = jnp.where(even, other[r].astype(F32), partner[r].astype(F32))
        elif r < rows + half:
            row = field[r - half].astype(F32)
        else:
            k = r - rows - half
            row = jnp.where(even, partner[k].astype(F32), other[k].astype(F32))
        ext[r, EDGE : EDGE + zonal, :] = row
        ext[r, EDGE - half : EDGE, :] = row[zonal - half :]
        ext[r, EDGE + zonal : EDGE + zonal + half, :] = row[:half]
    for start in range(0, zonal, STRIP):
        total = jnp.zeros((rows, STRIP, field.shape[2]), F32)
        for b in range(STENCIL_SIDE):
            first = EDGE - half + b + start
            slab = ext[:, first : first + STRIP, :]
            for a in range(STENCIL_SIDE):
                k = a * STENCIL_SIDE + b
                total = total + taps[k : k + 1, :][None] * slab[a : a + rows]
        centred = total - jnp.mean(total, axis=-1, keepdims=True)
        recip = lax.rsqrt(jnp.mean(centred * centred, axis=-1, keepdims=True) + EPSILON)
        value = centred * recip
        rounded = (gain[...][None] * value).astype(BF16)
        wide = jnp.broadcast_to(recip, value.shape)
        for i in range(rows):
            at = pl.ds(i * zonal + start, STRIP)
            scaled[at, :] = value[i]
            inverse[at, :] = wide[i]
            normed[at, :] = rounded[i]


def selector(rows, columns, chunk_bits, offsets, turned):
    place = lax.broadcasted_iota(jnp.int32, (rows, columns), 1 if turned else 0)
    variable = lax.broadcasted_iota(jnp.int32, (rows, columns), 0 if turned else 1)
    chunk = lax.shift_right_logical(place, chunk_bits)
    inside = place & ((1 << chunk_bits) - 1)
    result = jnp.zeros((rows, columns), F32)
    for offset in offsets:
        j = inside - offset
        hit = (j >= 0) & (j < PER_CHUNK) & (chunk * PER_CHUNK + j == variable)
        result = jnp.where(hit, 1.0, result)
    return result.astype(BF16)


def matrices(shards):
    count, owned, channels = shards.shape[0], shards.shape[1] // 2, shards.shape[2]
    return (
        shards[:, :owned, :].reshape(count * owned, channels),
        shards[:, owned:, :].reshape(count * owned, channels),
    )


def mlp_body(normed, mine, theirs, field, readout, gated, upper, residual, chunks):
    points, channels = normed.shape
    halves = [matrices(mine), matrices(theirs)]
    wide = upper.shape[1] // 2
    for k, (widen, _) in enumerate(halves):
        upper[:, k * wide : (k + 1) * wide] = dot(normed[...], widen, (1, 1))

    def step(i, carry):
        at = pl.ds(pl.multiple_of(i * 16, 16), 16)
        gated[at, :] = gelu_value(upper[at, :]).astype(BF16)
        return carry

    lax.fori_loop(0, points // 16, step, 0, unroll=2)
    mixed = sum(
        dot(gated[:, k * wide : (k + 1) * wide], shrink, (1, 0))
        for k, (_, shrink) in enumerate(halves)
    )
    residual[...] = (field[...].reshape(points, channels).astype(F32) + mixed).astype(BF16)
    members = chunks.shape[0]
    spread = dot(selector(members * CHUNK_ROWS, readout.shape[0], 3, (0,), False), readout[...], (1, 0))
    outlook = dot(spread.astype(BF16), residual[...], (1, 1))
    for e in range(members):
        chunks[e] = outlook[e * CHUNK_ROWS : (e + 1) * CHUNK_ROWS].astype(BF16)


def slope_body(upper, slope):
    def step(i, carry):
        at = pl.ds(pl.multiple_of(i * 16, 16), 16)
        slope[at, :] = gelu_slope(upper[at, :])
        return carry

    lax.fori_loop(0, upper.shape[0] // 16, step, 0, unroll=2)


def outlook_body(readout, residual, out):
    out[...] = dot(readout[...], residual[...], (1, 1)).astype(BF16)


def pair_body(place, everyone, truth, weight, payload, loss, rows, seen):
    member = place[1]
    members, _, points = everyone.shape
    variables, bands, lanes = truth.shape
    for j in range(PER_CHUNK):
        row = truth[jnp.minimum(member * PER_CHUNK + j, variables - 1)]
        for q in range(bands):
            seen[j : j + 1, q * lanes : (q + 1) * lanes] = row[q : q + 1]
    seen[PER_CHUNK:, :] = jnp.zeros((CHUNK_ROWS - PER_CHUNK, points), F32)
    limit = jnp.minimum(PER_CHUNK, variables - member * PER_CHUNK)
    real = lax.broadcasted_iota(jnp.int32, (CHUNK_ROWS, lanes), 0) < limit
    pair_norm = 1.0 / (members * (members - 1))
    lost = jnp.zeros((CHUNK_ROWS, lanes), F32)
    for q in range(points // lanes):
        at = slice(q * lanes, (q + 1) * lanes)
        y = [everyone[m, :, at].astype(F32) for m in range(members)]
        spread = [jnp.full((CHUNK_ROWS, lanes), SMOOTHING**0.5, F32) for _ in range(members)]
        ranks = [jnp.zeros((CHUNK_ROWS, lanes), F32) for _ in range(members)]
        for m in range(members):
            for k in range(m):
                gap = y[m] - y[k]
                square = gap * gap + SMOOTHING
                root = lax.rsqrt(square)
                size, tilt = square * root, gap * root
                spread[m], spread[k] = spread[m] + size, spread[k] + size
                ranks[m], ranks[k] = ranks[m] + tilt, ranks[k] - tilt
        scale = weight[0:1, at]
        for m in range(members):
            miss = y[m] - seen[:, at]
            square = miss * miss + SMOOTHING
            root = lax.rsqrt(square)
            term = scale * (square * root * (1.0 / members) - 0.5 * pair_norm * spread[m])
            lost = lost + jnp.where(real, term, 0.0)
            flow = scale * (miss * root * (1.0 / members) - pair_norm * ranks[m])
            average = spread[m] * (1.0 / (members - 1))
            high = average.astype(BF16).astype(F32)
            rows[m, 0:CHUNK_ROWS, at] = jnp.where(real, flow, 0.0)
            rows[m, PER_CHUNK : PER_CHUNK + CHUNK_ROWS, at] = high
            rows[m, 2 * PER_CHUNK : 16, at] = (average - high)[: 16 - 2 * PER_CHUNK]
    for m in range(members):
        payload[m] = rows[m].astype(BF16)
    loss[...] = jnp.sum(lost, axis=0, keepdims=True)


def average_body(back, out):
    members, height, points = back.shape
    pick = selector(out.shape[0], members * height, 4, (PER_CHUNK, 2 * PER_CHUNK), True)
    out[...] = dot(pick, back[...].reshape(members * height, points), (1, 0))


def backward_body(
    back, readout, residual, gated, slope, normed, scaled, inverse, gain, mine, theirs,
    widen_grad, shrink_grad, readout_grad, gain_grad, back_depth, gate, back_upper,
):
    members, height, points = back.shape
    halves = [matrices(mine), matrices(theirs)]
    wide = slope.shape[1] // 2
    flow = back[...].reshape(members * height, points)
    spread = dot(selector(members * height, readout.shape[0], 4, (0,), False), readout[...], (1, 0))
    back_residual = dot(flow, spread.astype(BF16), (0, 0)).astype(BF16)
    for k, (_, shrink) in enumerate(halves):
        gate[:, k * wide : (k + 1) * wide] = dot(back_residual, shrink, (1, 1))
    readout_grad[...] = dot(flow, residual[...], (1, 0))
    shrink_grad[...] = dot(gated[...], back_residual, (0, 0))

    def step(i, carry):
        at = pl.ds(pl.multiple_of(i * 16, 16), 16)
        back_upper[at, :] = (gate[at, :] * slope[at, :]).astype(BF16)
        return carry

    lax.fori_loop(0, points // 16, step, 0, unroll=2)
    back_norm = sum(
        dot(back_upper[:, k * wide : (k + 1) * wide], widen, (1, 0))
        for k, (widen, _) in enumerate(halves)
    )
    widen_grad[...] = dot(back_upper[...], normed[...], (0, 0))
    value = scaled[...]
    product = back_norm * value
    gain_grad[...] = jnp.sum(product, axis=0, keepdims=True)
    g = back_norm * gain[...]
    p = jnp.mean(g, axis=-1, keepdims=True)
    q = jnp.mean(g * value, axis=-1, keepdims=True)
    back_depth[...] = inverse[...] * (g - p - value * q)


def pack_body(back_depth, ext, widen_grad, shrink_grad, readout_grad, gain_grad, loss, send, keep, small):
    half = STENCIL_SIDE // 2
    zonal = ext.shape[1] - 2 * EDGE
    rows = back_depth.shape[0] // zonal
    channels = ext.shape[2]
    members = small.shape[0] // CHUNK_ROWS
    height = readout_grad.shape[0] // members
    small[TAPS_AT + 48 :, :] = jnp.zeros((small.shape[0] - TAPS_AT - 48, channels), F32)
    for e in range(members):
        count = min(PER_CHUNK, TAPS_AT - e * PER_CHUNK)
        if count > 0:
            small[e * PER_CHUNK : e * PER_CHUNK + count, :] = readout_grad[e * height : e * height + count, :]
    for b in range(STENCIL_SIDE):
        totals = [jnp.zeros((STRIP, channels), F32) for _ in range(STENCIL_SIDE)]
        for start in range(0, zonal, STRIP):
            first = EDGE - half + b + start
            slab = ext[:, first : first + STRIP, :]
            up = [back_depth[i * zonal + start : i * zonal + start + STRIP, :] for i in range(rows)]
            for a in range(STENCIL_SIDE):
                for i in range(rows):
                    totals[a] = totals[a] + up[i] * slab[i + a]
        for a in range(STENCIL_SIDE):
            k = TAPS_AT + a * STENCIL_SIDE + b
            small[k : k + 1, :] = jnp.sum(totals[a], axis=0, keepdims=True)
    small[TAPS_AT + 49 : TAPS_AT + 50, :] = gain_grad[...]
    small[TAPS_AT + 50 : TAPS_AT + 51, :] = loss[...]
    depth_z = DEPTH_Z
    for e in range(members):
        tail = small[e * CHUNK_ROWS : (e + 1) * CHUNK_ROWS, :]
        for h in range(2):
            d = 2 * e + h
            for mat, grad in enumerate((widen_grad, shrink_grad)):
                at = slice(mat * depth_z, (mat + 1) * depth_z)
                base = h * depth_z * members + e
                keep[d, at, :] = grad[pl.ds(base, depth_z, stride=members), :]
                base = base + 2 * depth_z * members
                send[d, at, :] = grad[pl.ds(base, depth_z, stride=members), :]
            keep[d, 2 * depth_z :, :] = tail
            send[d, 2 * depth_z :, :] = tail


def gradient_body(
    back, readout, residual, gated, slope, normed, scaled, inverse, gain, mine, theirs, ext, loss,
    send, keep, gate, back_upper, widen_grad, shrink_grad, readout_grad, gain_grad, back_depth, small,
):
    backward_body(
        back, readout, residual, gated, slope, normed, scaled, inverse, gain, mine, theirs,
        widen_grad, shrink_grad, readout_grad, gain_grad, back_depth, gate, back_upper,
    )
    pack_body(
        back_depth, ext, widen_grad, shrink_grad, readout_grad, gain_grad, loss,
        send, keep, small,
    )


def final_body(arrived, up, down, taps, gain, readout, loss, small):
    members = arrived.shape[0]
    for e in range(members):
        small[e * CHUNK_ROWS : (e + 1) * CHUNK_ROWS, :] = arrived[e, 0:CHUNK_ROWS, :]
        up[e : e + 1, :] = arrived[e, CHUNK_ROWS : CHUNK_ROWS + 1, :]
        down[e : e + 1, :] = arrived[e, CHUNK_ROWS + 1 : CHUNK_ROWS + 2, :]
    readout[...] = small[0:TAPS_AT, :]
    taps[...] = small[TAPS_AT : TAPS_AT + 49, :]
    gain[...] = small[TAPS_AT + 49 : TAPS_AT + 50, :]
    loss[...] = jnp.sum(small[TAPS_AT + 50 : TAPS_AT + 51, :], axis=1, keepdims=True)


def on_device(
    features,
    random_perturbation,
    observed_truth,
    stencil_taps,
    affine_factor,
    widen_matrix,
    shrink_matrix,
    readout_matrix,
):
    rows, zonal, channels = features.shape
    variables = readout_matrix.shape[0]
    half = STENCIL_SIDE // 2
    bands, members = lax.axis_size("lat"), lax.axis_size("ens")
    band, member = lax.axis_index("lat"), lax.axis_index("ens")
    points = rows * zonal
    latitudes = rows * bands
    hidden = widen_matrix.shape[0] * bands
    depth_z = DEPTH_Z
    share = CHUNK_ROWS
    place = jnp.stack([lax.rem(band, 2), member]).astype(jnp.int32)
    gain = affine_factor.reshape(1, channels)

    field = (features.astype(F32) + random_perturbation[0].astype(F32)).astype(BF16)
    partner, other = halo_rows(field, half)
    shape = (bands // 2,) + widen_matrix.shape
    pair = jnp.concatenate(
        [jnp.broadcast_to(widen_matrix[None], shape), jnp.broadcast_to(shrink_matrix[None], shape)],
        axis=1,
    )
    mine = exchange(pair, AXES, weight_groups(members, bands))
    mine, partner, other = lax.optimization_barrier((mine, partner, other))
    theirs = core_swap(mine)
    latitude = (band * rows + jnp.arange(points, dtype=jnp.int32) // zonal).astype(F32)
    area = jnp.cos(math.pi * ((latitude + 0.5) / latitudes - 0.5))
    weight = (area * (1.0 / (latitudes * zonal)))[None, :]

    wide = (rows + 2 * half, zonal + 2 * EDGE, channels)
    ext, scaled, inverse, normed = vmem_call(
        stencil_body,
        [
            (wide, F32),
            ((points, channels), F32),
            ((points, channels), F32),
            ((points, channels), BF16),
        ],
        scalars=1,
        vectors=5,
    )(place, field, partner, other, stencil_taps, gain)
    gated, upper, residual, chunks = vmem_call(
        mlp_body,
        [
            ((points, hidden), BF16),
            ((points, hidden), F32),
            ((points, channels), BF16),
            ((members, CHUNK_ROWS, points), BF16),
        ],
        vectors=5,
    )(normed, mine, theirs, field, readout_matrix)
    everyone = exchange(chunks, "ens")
    (slope,) = vmem_call(slope_body, [((points, hidden), F32)], vectors=1, aliases={0: 0})(upper)
    (outlook,) = vmem_call(outlook_body, [((variables, points), BF16)], vectors=2)(
        readout_matrix, residual
    )
    sample_outlook = outlook.reshape(1, variables, rows, zonal)
    payload, loss = vmem_call(
        pair_body,
        [((members, 16, points), BF16), ((1, zonal), F32)],
        [pltpu.VMEM((members, 16, points), F32), pltpu.VMEM((CHUNK_ROWS, points), F32)],
        scalars=1,
        vectors=3,
    )(place, everyone, observed_truth, weight)
    back = exchange(payload, "ens")
    (average,) = vmem_call(average_body, [((variables, points), F32)], vectors=1)(back)
    sample_average_spread = average.reshape(1, variables, rows, zonal)

    packet = ((2 * members, 2 * depth_z + share, channels), F32)
    send, keep = vmem_call(
        gradient_body,
        [packet, packet],
        [
            pltpu.VMEM((points, hidden), F32),
            pltpu.VMEM((points, hidden), BF16),
            pltpu.VMEM((hidden, channels), F32),
            pltpu.VMEM((hidden, channels), F32),
            pltpu.VMEM((members * 16, channels), F32),
            pltpu.VMEM((1, channels), F32),
            pltpu.VMEM((points, channels), F32),
            pltpu.VMEM((members * share, channels), F32),
        ],
        vectors=13,
    )(
        back, readout_matrix, residual, gated, slope, normed, scaled, inverse, gain, mine, theirs,
        ext, loss,
    )

    total = (keep + core_swap(send)).astype(BF16)
    arrived = exchange(total, AXES, plane_groups(members, bands)).astype(F32)
    columns = [
        list(range(h * bands // 2 + c, (h + 1) * bands // 2, 2)) for h in range(2) for c in range(2)
    ]
    part = jnp.sum(arrived, axis=0)
    outgoing = jnp.concatenate(
        [
            jnp.broadcast_to(part[None, 2 * depth_z :], (depth_z, share, channels)),
            part[: 2 * depth_z].reshape(2, depth_z, channels).transpose(1, 0, 2),
        ],
        axis=1,
    )
    done = jnp.sum(exchange(outgoing, "lat", columns), axis=0)
    arrived = exchange(jnp.broadcast_to(done[None], (members,) + done.shape), "ens")
    up, down, taps, gain_total, readout, loss = vmem_call(
        final_body,
        [
            ((members, channels), F32),
            ((members, channels), F32),
            ((STENCIL_SIDE * STENCIL_SIDE, channels), F32),
            ((1, channels), F32),
            ((variables, channels), F32),
            ((1, 1), F32),
        ],
        [pltpu.VMEM((members * share, channels), F32)],
        vectors=1,
        kept=range(6),
    )(arrived)
    return (
        loss.reshape(()),
        taps,
        gain_total.reshape(channels),
        up,
        down,
        readout,
        sample_outlook,
        sample_average_spread,
    )


def solution(mesh):
    in_specs = (
        P("lat", None, None),
        P("ens", "lat", None, None),
        P(None, "lat", None),
        P(),
        P(),
        P("lat", None),
        P("lat", None),
        P(),
    )
    out_specs = (
        P(),
        P(),
        P(),
        P("lat", None),
        P("lat", None),
        P(),
        P("ens", None, "lat", None),
        P("ens", None, "lat", None),
    )

    return jax.shard_map(
        on_device, mesh=mesh, in_specs=in_specs, out_specs=out_specs, check_vma=False
    )
```

profile of v0, /device:TPU:8, one launch (start us, length us, event | category | flops | bytes accessed | tf_op | source)
XLA Modules:
  0.0 118.6 jit_solution(18425797644943716499)
XLA Ops:
  0.6 0.0 copy-start.8
  0.6 0.7 broadcast_in_dim.8
  1.3 0.0 copy-done.8
  1.4 0.7 pad_maximum_fusion
  2.0 0.0 copy-start.6
  2.0 0.0 copy-start.7
  2.0 13.3 %all-to-all-start = ((bf16[16,32,128]{2,1,0:T(8,128)(2,1)}), bf16[16,32,128]{2,1,0:T(8,128)(2,1)S(1)}, u32[]{:S(2)}, u32[]{:S(2)}) async-start(bf16[16,32,128]{2,1,0:T(8,128)(2,1)} %pad_maximum_fusion), calls=%async_computation | async-start | bytes 262144 | tf_op jit(solution)/shard_map/all_to_all | solution.py:42
  15.4 0.0 copy-done.6
  15.4 0.0 copy-done.7
  15.5 0.0 copy-start.4
  15.5 1.9 %collective-permute-start = (bf16[3,128,128]{2,1,0:T(8,128)(2,1)S(1)}, bf16[3,128,128]{2,1,0:T(8,128)(2,1)S(1)}, u32[]{:S(2)}, u32[]{:S(2)}) collective-permute-start(bf16[3,128,128]{2,1,0:T(8,128)(2,1)S(1)} %get-tuple-element.51), channel_id=1, source_target_pairs={{0,1},{1,0},{2,3},{3,2},{4,5},{5,4},{6,7},{7,6},{8,9},{9,8},{10,11... | collective-permute-start | bytes 294920 | tf_op jit(solution)/shard_map/ppermute | solution.py:26
  17.4 0.7 collective-permute-start.1
  18.1 0.6 collective-permute-done.partner
  18.7 0.0 collective-permute-done.1.other
  18.7 7.4 %all-to-all-done.mine = bf16[16,32,128]{2,1,0:T(8,128)(2,1)S(1)} async-done(((bf16[16,32,128]{2,1,0:T(8,128)(2,1)}), bf16[16,32,128]{2,1,0:T(8,128)(2,1)S(1)}, u32[]{:S(2)}, u32[]{:S(2)}) %all-to-all-start) | async-done | bytes 131104 | tf_op jit(solution)/shard_map/all_to_all | solution.py:42
  26.1 1.9 %collective-permute-start.2 = (bf16[16,32,128]{2,1,0:T(8,128)(2,1)S(1)}, bf16[16,32,128]{2,1,0:T(8,128)(2,1)S(1)}, u32[]{:S(2)}, u32[]{:S(2)}) collective-permute-start(bf16[16,32,128]{2,1,0:T(8,128)(2,1)S(1)} %all-to-all-done.mine), channel_id=1, source_target_pairs={{0,1},{1,0},{2,3},{3,2},{4,5},{5,4},{6,7},{7,6},{8,9},{9,8},{10,11... | collective-permute-start | bytes 393224 | tf_op jit(solution)/shard_map/ppermute | solution.py:26
  28.1 0.1 pad_add_fusion.place
  28.1 0.0 copy-start.5
  28.1 0.0 copy-done.4
  28.1 0.7 copy-done.5
  28.8 0.0 copy-start.2
  28.8 1.8 %shard_map.143 = (f32[10,144,128]{2,1,0:T(8,128)S(1)}, f32[512,128]{1,0:T(8,128)S(1)}, f32[512,128]{1,0:T(8,128)S(1)}, bf16[512,128]{1,0:T(8,128)(2,1)S(1)}) custom-call(s32[2]{0:T(128)S(1)} %pad_add_fusion.place, bf16[4,128,128]{2,1,0:T(8,128)(2,1)S(1)} %fusion.field, bf16[3,128,128]{2,1,0:T(8,128)(2,1)S(1)} %collective-permute-done.partner, ...), custom_call_target="tpu_custom_call" | custom-call | tf_op jit(solution)/shard_map/pallas_call | solution.py:101
  30.6 0.0 copy-start
  30.6 0.7 copy-done
  31.3 0.0 collective-permute-done.2.theirs
  31.3 0.0 copy-done.2
  31.3 1.9 %shard_map.144 = (bf16[512,512]{1,0:T(8,128)(2,1)S(1)}, f32[512,512]{1,0:T(8,128)S(1)}, bf16[512,128]{1,0:T(8,128)(2,1)S(1)}, bf16[16,8,512]{2,1,0:T(8,128)(2,1)}) custom-call(bf16[512,128]{1,0:T(8,128)(2,1)S(1)} %get-tuple-element.31.normed, bf16[16,32,128]{2,1,0:T(8,128)(2,1)S(1)} %all-to-all-done.mine, ...), custom_call_target="tpu_custom_call" | custom-call | tf_op jit(solution)/shard_map/pallas_call | solution.py:101
  33.2 0.0 copy-start.3
  33.2 7.7 %all-to-all-start.1 = ((bf16[16,8,512]{2,1,0:T(8,128)(2,1)}), bf16[16,8,512]{2,1,0:T(8,128)(2,1)S(1)}, u32[]{:S(2)}, u32[]{:S(2)}) async-start(bf16[16,8,512]{2,1,0:T(8,128)(2,1)} %get-tuple-element.33), calls=%async_computation.1 | async-start | bytes 262144 | tf_op jit(solution)/shard_map/all_to_all | solution.py:42
  40.9 0.1 fusion.8.weight
  41.0 7.5 %all-to-all-done.1.everyone = bf16[16,8,512]{2,1,0:T(8,128)(2,1)S(1)} async-done(((bf16[16,8,512]{2,1,0:T(8,128)(2,1)}), bf16[16,8,512]{2,1,0:T(8,128)(2,1)S(1)}, u32[]{:S(2)}, u32[]{:S(2)}) %all-to-all-start.1) | async-done | bytes 131104 | tf_op jit(solution)/shard_map/all_to_all | solution.py:42
  48.5 0.0 copy-done.3
  48.5 2.1 %shard_map.145 = (bf16[16,16,512]{2,1,0:T(8,128)(2,1)}, f32[1,128]{1,0:T(1,128)S(1)}) custom-call(s32[2]{0:T(128)S(1)} %pad_add_fusion.place, bf16[16,8,512]{2,1,0:T(8,128)(2,1)S(1)} %all-to-all-done.1.everyone, f32[69,4,128]{2,1,0:T(4,128)S(1)} %copy-done.3, f32[1,512]{1,0:T(1,128)S(1)} %fusion.8.weight), custom_call_target="tpu_custom_call" | custom-call | tf_op jit(solution)/shard_map/pallas_call | solution.py:101
  50.7 4.6 %all-to-all-start.2 = ((bf16[16,16,512]{2,1,0:T(8,128)(2,1)}), bf16[16,16,512]{2,1,0:T(8,128)(2,1)S(1)}, u32[]{:S(2)}, u32[]{:S(2)}) async-start(bf16[16,16,512]{2,1,0:T(8,128)(2,1)} %get-tuple-element.34), calls=%async_computation.2 | async-start | bytes 524288 | tf_op jit(solution)/shard_map/all_to_all | solution.py:42
  55.2 0.8 shard_map.146.slope
  56.0 8.2 %all-to-all-done.2.back = bf16[16,16,512]{2,1,0:T(8,128)(2,1)S(1)} async-done(((bf16[16,16,512]{2,1,0:T(8,128)(2,1)}), bf16[16,16,512]{2,1,0:T(8,128)(2,1)S(1)}, u32[]{:S(2)}, u32[]{:S(2)}) %all-to-all-start.2) | async-done | bytes 262176 | tf_op jit(solution)/shard_map/all_to_all | solution.py:42
  64.2 0.0 copy-start.1
  64.2 0.9 copy-done.1
  65.1 3.1 %shard_map.147 = (f32[32,24,128]{2,1,0:T(8,128)S(1)}, f32[32,24,128]{2,1,0:T(8,128)S(1)}) custom-call(bf16[16,16,512]{2,1,0:T(8,128)(2,1)S(1)} %all-to-all-done.2.back, bf16[69,128]{1,0:T(8,128)(2,1)S(1)} %copy-done.2, bf16[512,128]{1,0:T(8,128)(2,1)S(1)} %get-tuple-element.35.residual, bf16[512,512]{1,0:T(8,128)(2,1)S(1)} %get-tuple-element.36.gated, ...), custom_call_target="tpu_custom_call" | custom-call | tf_op jit(solution)/shard_map/pallas_call | solution.py:101
  68.2 1.9 %collective-permute-start.3 = (f32[32,24,128]{2,1,0:T(8,128)S(1)}, f32[32,24,128]{2,1,0:T(8,128)S(1)}, u32[]{:S(2)}, u32[]{:S(2)}) collective-permute-start(f32[32,24,128]{2,1,0:T(8,128)S(1)} %get-tuple-element.43), channel_id=1, source_target_pairs={{0,1},{1,0},{2,3},{3,2},{4,5},{5,4},{6,7},{7,6},{8,9},{9,8},{10,11... | collective-permute-start | bytes 1179656 | tf_op jit(solution)/shard_map/ppermute | solution.py:26
  70.2 1.7 %collective-permute-done.3 = f32[32,24,128]{2,1,0:T(8,128)S(1)} collective-permute-done((f32[32,24,128]{2,1,0:T(8,128)S(1)}, f32[32,24,128]{2,1,0:T(8,128)S(1)}, u32[]{:S(2)}, u32[]{:S(2)}) %collective-permute-start.3) | collective-permute-done | bytes 393248 | tf_op jit(solution)/shard_map/ppermute | solution.py:26
  71.9 0.1 add_convert_fusion
  71.9 22.4 %all_to_all.30 = bf16[32,24,128]{2,1,0:T(8,128)(2,1)S(1)} all-to-all(bf16[32,24,128]{2,1,0:T(8,128)(2,1)S(1)} %add_convert_fusion), channel_id=1, replica_groups={{0,16,32,48,64,80,96,112,128,144,160,176,192,208,224,240,256,272,288,30..., dimensions={0} | all-to-all | bytes 393216 | tf_op jit(solution)/shard_map/all_to_all | solution.py:42
  94.4 10.8 %all_to_all.31 = f32[8,10,128]{2,1,0:T(8,128)S(1)} all-to-all(f32[8,10,128]{2,1,0:T(8,128)S(1)} %pad_maximum_fusion.1), channel_id=1, replica_groups={{0,2,4,6,8,10,12,14},{1,3,5,7,9,11,13,15},{16,18,20,22,24,26,28,30},{17..., dimensions={0} | all-to-all | bytes 81920 | tf_op jit(solution)/shard_map/all_to_all | solution.py:42
  105.2 0.7 broadcast_in_dim.11
  105.8 4.8 %all-to-all-start.5 = ((f32[16,10,128]{2,1,0:T(8,128)}), f32[16,10,128]{2,1,0:T(8,128)S(1)}, u32[]{:S(2)}, u32[]{:S(2)}) async-start(f32[16,10,128]{2,1,0:T(8,128)} %broadcast_in_dim.11), calls=%async_computation.5 | async-start | bytes 262144 | tf_op jit(solution)/shard_map/all_to_all | solution.py:42
  110.6 0.2 shard_map.149
  110.7 0.7 reshape.102
  111.4 0.2 shard_map.150
  111.6 0.7 reshape.103
  112.3 5.6 %all-to-all-done.5.arrived = f32[16,10,128]{2,1,0:T(8,128)S(1)} async-done(((f32[16,10,128]{2,1,0:T(8,128)}), f32[16,10,128]{2,1,0:T(8,128)S(1)}, u32[]{:S(2)}, u32[]{:S(2)}) %all-to-all-start.5) | async-done | bytes 81952 | tf_op jit(solution)/shard_map/all_to_all | solution.py:42
  117.9 0.7 shard_map.148
  (10 shorter events, 0.1 us)
Async XLA Ops:
  0.6 0.7 copy-start.8
  2.0 13.4 %copy-start.6 = (bf16[4,128,128]{2,1,0:T(8,128)(2,1)S(1)}, bf16[4,128,128]{2,1,0:T(8,128)(2,1)}, u32[]{:S(2)}) copy-start(bf16[4,128,128]{2,1,0:T(8,128)(2,1)} %param.8) | copy-start | bytes 393220
  2.0 13.4 %copy-start.7 = (bf16[1,4,128,128]{3,2,1,0:T(8,128)(2,1)S(1)}, bf16[1,4,128,128]{3,2,1,0:T(8,128)(2,1)}, u32[]{:S(2)}) copy-start(bf16[1,4,128,128]{3,2,1,0:T(8,128)(2,1)} %param.9) | copy-start | bytes 393220
  2.0 24.1 %all-to-all-start = ((bf16[16,32,128]{2,1,0:T(8,128)(2,1)}), bf16[16,32,128]{2,1,0:T(8,128)(2,1)S(1)}, u32[]{:S(2)}, u32[]{:S(2)}) async-start(bf16[16,32,128]{2,1,0:T(8,128)(2,1)} %pad_maximum_fusion), calls=%async_computation | async-start | bytes 262144 | tf_op jit(solution)/shard_map/all_to_all | solution.py:42
  15.5 12.7 %copy-start.4 = (f32[49,128]{1,0:T(8,128)S(1)}, f32[49,128]{1,0:T(8,128)}, u32[]{:S(2)}) copy-start(f32[49,128]{1,0:T(8,128)} %taps.1) | copy-start | bytes 75268
  15.5 3.2 %collective-permute-start = (bf16[3,128,128]{2,1,0:T(8,128)(2,1)S(1)}, bf16[3,128,128]{2,1,0:T(8,128)(2,1)S(1)}, u32[]{:S(2)}, u32[]{:S(2)}) collective-permute-start(bf16[3,128,128]{2,1,0:T(8,128)(2,1)S(1)} %get-tuple-element.51), channel_id=1, source_target_pairs={{0,1},{1,0},{2,3},{3,2},{4,5},{5,4},{6,7},{7,6},{8,9},{9,8},{10,11... | collective-permute-start | bytes 294920 | tf_op jit(solution)/shard_map/ppermute | solution.py:26
  17.4 1.3 %collective-permute-start.1 = (bf16[3,128,128]{2,1,0:T(8,128)(2,1)S(1)}, bf16[3,128,128]{2,1,0:T(8,128)(2,1)S(1)}, u32[]{:S(2)}, u32[]{:S(2)}) collective-permute-start(bf16[3,128,128]{2,1,0:T(8,128)(2,1)S(1)} %get-tuple-element.50), channel_id=1, source_target_pairs={{1,2},{3,4},{5,6},{7,8},{9,10},{11,12},{13,14},{15,16},{17,18},{19... | collective-permute-start | bytes 294920 | tf_op jit(solution)/shard_map/ppermute | solution.py:32
  26.1 5.1 %collective-permute-start.2 = (bf16[16,32,128]{2,1,0:T(8,128)(2,1)S(1)}, bf16[16,32,128]{2,1,0:T(8,128)(2,1)S(1)}, u32[]{:S(2)}, u32[]{:S(2)}) collective-permute-start(bf16[16,32,128]{2,1,0:T(8,128)(2,1)S(1)} %all-to-all-done.mine), channel_id=1, source_target_pairs={{0,1},{1,0},{2,3},{3,2},{4,5},{5,4},{6,7},{7,6},{8,9},{9,8},{10,11... | collective-permute-start | bytes 393224 | tf_op jit(solution)/shard_map/ppermute | solution.py:26
  28.1 0.7 copy-start.5
  28.8 2.5 %copy-start.2 = (bf16[69,128]{1,0:T(8,128)(2,1)S(1)}, bf16[69,128]{1,0:T(8,128)(2,1)}, u32[]{:S(2)}) copy-start(bf16[69,128]{1,0:T(8,128)(2,1)} %readout.5) | copy-start | bytes 52996
  30.6 0.7 copy-start
  33.2 15.3 %copy-start.3 = (f32[69,4,128]{2,1,0:T(4,128)S(1)}, f32[69,4,128]{2,1,0:T(4,128)}, u32[]{:S(2)}) copy-start(f32[69,4,128]{2,1,0:T(4,128)} %truth.1) | copy-start | bytes 423940
  33.2 15.3 %all-to-all-start.1 = ((bf16[16,8,512]{2,1,0:T(8,128)(2,1)}), bf16[16,8,512]{2,1,0:T(8,128)(2,1)S(1)}, u32[]{:S(2)}, u32[]{:S(2)}) async-start(bf16[16,8,512]{2,1,0:T(8,128)(2,1)} %get-tuple-element.33), calls=%async_computation.1 | async-start | bytes 262144 | tf_op jit(solution)/shard_map/all_to_all | solution.py:42
  50.7 13.5 %all-to-all-start.2 = ((bf16[16,16,512]{2,1,0:T(8,128)(2,1)}), bf16[16,16,512]{2,1,0:T(8,128)(2,1)S(1)}, u32[]{:S(2)}, u32[]{:S(2)}) async-start(bf16[16,16,512]{2,1,0:T(8,128)(2,1)} %get-tuple-element.34), calls=%async_computation.2 | async-start | bytes 524288 | tf_op jit(solution)/shard_map/all_to_all | solution.py:42
  64.2 1.0 copy-start.1
  68.2 3.6 %collective-permute-start.3 = (f32[32,24,128]{2,1,0:T(8,128)S(1)}, f32[32,24,128]{2,1,0:T(8,128)S(1)}, u32[]{:S(2)}, u32[]{:S(2)}) collective-permute-start(f32[32,24,128]{2,1,0:T(8,128)S(1)} %get-tuple-element.43), channel_id=1, source_target_pairs={{0,1},{1,0},{2,3},{3,2},{4,5},{5,4},{6,7},{7,6},{8,9},{9,8},{10,11... | collective-permute-start | bytes 1179656 | tf_op jit(solution)/shard_map/ppermute | solution.py:26
  105.8 12.1 %all-to-all-start.5 = ((f32[16,10,128]{2,1,0:T(8,128)}), f32[16,10,128]{2,1,0:T(8,128)S(1)}, u32[]{:S(2)}, u32[]{:S(2)}) async-start(f32[16,10,128]{2,1,0:T(8,128)} %broadcast_in_dim.11), calls=%async_computation.5 | async-start | bytes 262144 | tf_op jit(solution)/shard_map/all_to_all | solution.py:42
where the time goes:
time: 119 us
  starting transfers between devices  36.8 us (31%)
  blocking collectives  33.1 us (28%)
  waiting for transfers between devices  31 us (26%)
  Pallas kernels  10.7 us (9%)
  local copies, waits for them, and re-layouts  5.11 us (4%)
    all_to_all x2, blocking collectives, exchange(): lax.all_to_all(value, axis, 0, 0, tiled=True, axis_index_groups=groups)  33.1 us
    all_to_all x4, starting transfers between devices, exchange(): lax.all_to_all(value, axis, 0, 0, tiled=True, axis_index_groups=groups)  30.4 us
    all_to_all x4, waiting for transfers between devices, exchange(): lax.all_to_all(value, axis, 0, 0, tiled=True, axis_index_groups=groups)  28.7 us
    pallas_call x8, Pallas kernels, run(): return call(*operands)  10.7 us
    ppermute x3, starting transfers between devices, core_swap(): return lax.ppermute(value, 'lat', [(i, i ^ 1) for i in range(count)])  5.75 us
  transfers between devices with their start and end apart: 8, of which 6 were waited for; matrix products, arithmetic and copies ran while one was open for 1% of the time, Pallas kernels for 2%

commit v1 on v0

--- a/solution.py
+++ b/solution.py
@@ -107,7 +107,7 @@
     return lax.dot_general(a, b, ((contract[:1], contract[1:]), ((), ())), preferred_element_type=F32)
 
 
-def stencil_body(place, field, partner, other, taps, gain, ext, scaled, inverse, normed):
+def fill_rows(place, field, partner, other, ext):
     even = place[0] == 0
     rows, zonal, _ = field.shape
     half = STENCIL_SIDE // 2
@@ -122,6 +122,12 @@
         ext[r, EDGE : EDGE + zonal, :] = row
         ext[r, EDGE - half : EDGE, :] = row[zonal - half :]
         ext[r, EDGE + zonal : EDGE + zonal + half, :] = row[:half]
+
+
+def stencil_body(place, field, partner, other, taps, gain, scaled, inverse, normed, ext):
+    rows, zonal, _ = field.shape
+    half = STENCIL_SIDE // 2
+    fill_rows(place, field, partner, other, ext)
     for start in range(0, zonal, STRIP):
         total = jnp.zeros((rows, STRIP, field.shape[2]), F32)
         for b in range(STENCIL_SIDE):
@@ -204,9 +210,11 @@
 def pair_body(place, everyone, truth, weight, payload, loss, rows, seen):
     member = place[1]
     members, _, points = everyone.shape
-    variables, bands, lanes = truth.shape
+    _, bands, lanes = truth.shape
+    variables = TAPS_AT
+    first = jnp.minimum(member * PER_CHUNK, variables - PER_CHUNK)
     for j in range(PER_CHUNK):
-        row = truth[jnp.minimum(member * PER_CHUNK + j, variables - 1)]
+        row = truth[jnp.minimum(member * PER_CHUNK + j, variables - 1) - first]
         for q in range(bands):
             seen[j : j + 1, q * lanes : (q + 1) * lanes] = row[q : q + 1]
     seen[PER_CHUNK:, :] = jnp.zeros((CHUNK_ROWS - PER_CHUNK, points), F32)
@@ -328,9 +336,10 @@
 
 
 def gradient_body(
-    back, readout, residual, gated, slope, normed, scaled, inverse, gain, mine, theirs, ext, loss,
-    send, keep, gate, back_upper, widen_grad, shrink_grad, readout_grad, gain_grad, back_depth, small,
+    place, back, readout, residual, gated, slope, normed, scaled, inverse, gain, mine, theirs, loss,
+    field, partner, other, send, keep, ext, gate, back_upper, widen_grad, shrink_grad, readout_grad, gain_grad, back_depth, small,
 ):
+    fill_rows(place, field, partner, other, ext)
     backward_body(
         back, readout, residual, gated, slope, normed, scaled, inverse, gain, mine, theirs,
         widen_grad, shrink_grad, readout_grad, gain_grad, back_depth, gate, back_upper,
@@ -391,14 +400,14 @@
     weight = (area * (1.0 / (latitudes * zonal)))[None, :]
 
     wide = (rows + 2 * half, zonal + 2 * EDGE, channels)
-    ext, scaled, inverse, normed = vmem_call(
+    scaled, inverse, normed = vmem_call(
         stencil_body,
         [
-            (wide, F32),
             ((points, channels), F32),
             ((points, channels), F32),
             ((points, channels), BF16),
         ],
+        [pltpu.VMEM(wide, F32)],
         scalars=1,
         vectors=5,
     )(place, field, partner, other, stencil_taps, gain)
@@ -414,6 +423,8 @@
     )(normed, mine, theirs, field, readout_matrix)
     everyone = exchange(chunks, "ens")
     (slope,) = vmem_call(slope_body, [((points, hidden), F32)], vectors=1, aliases={0: 0})(upper)
+    first = jnp.minimum(member * PER_CHUNK, variables - PER_CHUNK)
+    truth = lax.dynamic_slice_in_dim(observed_truth, first, PER_CHUNK, axis=0)
     (outlook,) = vmem_call(outlook_body, [((variables, points), BF16)], vectors=2)(
         readout_matrix, residual
     )
@@ -424,7 +435,7 @@
         [pltpu.VMEM((members, 16, points), F32), pltpu.VMEM((CHUNK_ROWS, points), F32)],
         scalars=1,
         vectors=3,
-    )(place, everyone, observed_truth, weight)
+    )(place, everyone, truth, weight)
     back = exchange(payload, "ens")
     (average,) = vmem_call(average_body, [((variables, points), F32)], vectors=1)(back)
     sample_average_spread = average.reshape(1, variables, rows, zonal)
@@ -434,6 +445,7 @@
         gradient_body,
         [packet, packet],
         [
+            pltpu.VMEM(wide, F32),
             pltpu.VMEM((points, hidden), F32),
             pltpu.VMEM((points, hidden), BF16),
             pltpu.VMEM((hidden, channels), F32),
@@ -443,10 +455,11 @@
             pltpu.VMEM((points, channels), F32),
             pltpu.VMEM((members * share, channels), F32),
         ],
-        vectors=13,
+        scalars=1,
+        vectors=15,
     )(
-        back, readout_matrix, residual, gated, slope, normed, scaled, inverse, gain, mine, theirs,
-        ext, loss,
+        place, back, readout_matrix, residual, gated, slope, normed, scaled, inverse, gain, mine,
+        theirs, loss, field, partner, other,
     )
 
     total = (keep + core_swap(send)).astype(BF16)

time: 119 us -> 118 us (level)
  transfers between devices with their start and end apart: 8 -> 8, of which waited for: 6 -> 6; matrix products, arithmetic and copies ran while one was open for 1% -> 1% of each run, Pallas kernels for 2% -> 3%
where the time goes in v1:
time: 118 us
  starting transfers between devices  36.6 us (31%)
  blocking collectives  33.1 us (28%)
  waiting for transfers between devices  31 us (26%)
  Pallas kernels  10.9 us (9%)
  local copies, waits for them, and re-layouts  4.22 us (4%)
    all_to_all x2, blocking collectives, exchange(): lax.all_to_all(value, axis, 0, 0, tiled=True, axis_index_groups=groups)  33.1 us
    all_to_all x4, starting transfers between devices, exchange(): lax.all_to_all(value, axis, 0, 0, tiled=True, axis_index_groups=groups)  30.2 us
    all_to_all x4, waiting for transfers between devices, exchange(): lax.all_to_all(value, axis, 0, 0, tiled=True, axis_index_groups=groups)  28.7 us
    pallas_call x8, Pallas kernels, run(): return call(*operands)  10.9 us
    ppermute x3, starting transfers between devices, core_swap(): return lax.ppermute(value, 'lat', [(i, i ^ 1) for i in range(count)])  5.75 us
  transfers between devices with their start and end apart: 8, of which 6 were waited for; matrix products, arithmetic and copies ran while one was open for 1% of the time, Pallas kernels for 3%

profile of v1, /device:TPU:8, one launch (start us, length us, event | category | flops | bytes accessed | tf_op | source)
XLA Modules:
  0.0 117.7 jit_solution(9045400824742708144)
XLA Ops:
  0.6 0.0 copy-start
  0.6 0.0 copy-start.7
  0.7 0.7 broadcast_in_dim.8
  1.4 0.0 copy-done.7
  1.4 0.7 pad_maximum_fusion
  2.1 0.0 copy-start.5
  2.1 0.0 copy-start.6
  2.1 13.3 %all-to-all-start = ((bf16[16,32,128]{2,1,0:T(8,128)(2,1)}), bf16[16,32,128]{2,1,0:T(8,128)(2,1)S(1)}, u32[]{:S(2)}, u32[]{:S(2)}) async-start(bf16[16,32,128]{2,1,0:T(8,128)(2,1)} %pad_maximum_fusion), calls=%async_computation | async-start | bytes 262144 | tf_op jit(solution)/shard_map/all_to_all | solution.py:42
  15.5 0.0 copy-done.5
  15.5 0.0 copy-done.6
  15.5 0.0 copy-start.3
  15.6 1.9 %collective-permute-start = (bf16[3,128,128]{2,1,0:T(8,128)(2,1)S(1)}, bf16[3,128,128]{2,1,0:T(8,128)(2,1)S(1)}, u32[]{:S(2)}, u32[]{:S(2)}) collective-permute-start(bf16[3,128,128]{2,1,0:T(8,128)(2,1)S(1)} %get-tuple-element.49), channel_id=1, source_target_pairs={{0,1},{1,0},{2,3},{3,2},{4,5},{5,4},{6,7},{7,6},{8,9},{9,8},{10,11... | collective-permute-start | bytes 294920 | tf_op jit(solution)/shard_map/ppermute | solution.py:26
  17.5 0.7 collective-permute-start.1
  18.2 0.6 collective-permute-done.partner
  18.8 0.0 collective-permute-done.1.other
  18.8 7.4 %all-to-all-done.mine = bf16[16,32,128]{2,1,0:T(8,128)(2,1)S(1)} async-done(((bf16[16,32,128]{2,1,0:T(8,128)(2,1)}), bf16[16,32,128]{2,1,0:T(8,128)(2,1)S(1)}, u32[]{:S(2)}, u32[]{:S(2)}) %all-to-all-start) | async-done | bytes 131104 | tf_op jit(solution)/shard_map/all_to_all | solution.py:42
  26.2 1.9 %collective-permute-start.2 = (bf16[16,32,128]{2,1,0:T(8,128)(2,1)S(1)}, bf16[16,32,128]{2,1,0:T(8,128)(2,1)S(1)}, u32[]{:S(2)}, u32[]{:S(2)}) collective-permute-start(bf16[16,32,128]{2,1,0:T(8,128)(2,1)S(1)} %all-to-all-done.mine), channel_id=1, source_target_pairs={{0,1},{1,0},{2,3},{3,2},{4,5},{5,4},{6,7},{7,6},{8,9},{9,8},{10,11... | collective-permute-start | bytes 393224 | tf_op jit(solution)/shard_map/ppermute | solution.py:26
  28.1 0.1 pad_add_fusion.place
  28.2 0.0 copy-start.4
  28.2 0.0 copy-done.3
  28.2 0.7 copy-done.4
  28.9 0.0 copy-start.2
  28.9 2.0 %shard_map.143 = (f32[512,128]{1,0:T(8,128)S(1)}, f32[512,128]{1,0:T(8,128)S(1)}, bf16[512,128]{1,0:T(8,128)(2,1)S(1)}) custom-call(s32[2]{0:T(128)S(1)} %pad_add_fusion.place, bf16[4,128,128]{2,1,0:T(8,128)(2,1)S(1)} %fusion.field, bf16[3,128,128]{2,1,0:T(8,128)(2,1)S(1)} %collective-permute-done.partner, ...), custom_call_target="tpu_custom_call" | custom-call | tf_op jit(solution)/shard_map/pallas_call | solution.py:101
  30.8 0.0 collective-permute-done.2.theirs
  30.9 0.0 copy-done.2
  30.9 1.9 %shard_map.144 = (bf16[512,512]{1,0:T(8,128)(2,1)S(1)}, f32[512,512]{1,0:T(8,128)S(1)}, bf16[512,128]{1,0:T(8,128)(2,1)S(1)}, bf16[16,8,512]{2,1,0:T(8,128)(2,1)}) custom-call(bf16[512,128]{1,0:T(8,128)(2,1)S(1)} %get-tuple-element.30.normed, bf16[16,32,128]{2,1,0:T(8,128)(2,1)S(1)} %all-to-all-done.mine, ...), custom_call_target="tpu_custom_call" | custom-call | tf_op jit(solution)/shard_map/pallas_call | solution.py:101
  32.8 7.6 %all-to-all-start.1 = ((bf16[16,8,512]{2,1,0:T(8,128)(2,1)}), bf16[16,8,512]{2,1,0:T(8,128)(2,1)S(1)}, u32[]{:S(2)}, u32[]{:S(2)}) async-start(bf16[16,8,512]{2,1,0:T(8,128)(2,1)} %get-tuple-element.32), calls=%async_computation.1 | async-start | bytes 262144 | tf_op jit(solution)/shard_map/all_to_all | solution.py:42
  40.4 0.1 fusion.8.weight
  40.5 0.0 copy-done
  40.5 7.5 %all-to-all-done.1.everyone = bf16[16,8,512]{2,1,0:T(8,128)(2,1)S(1)} async-done(((bf16[16,8,512]{2,1,0:T(8,128)(2,1)}), bf16[16,8,512]{2,1,0:T(8,128)(2,1)S(1)}, u32[]{:S(2)}, u32[]{:S(2)}) %all-to-all-start.1) | async-done | bytes 131104 | tf_op jit(solution)/shard_map/all_to_all | solution.py:42
  48.0 1.5 %shard_map.145 = (bf16[16,16,512]{2,1,0:T(8,128)(2,1)S(1)}, f32[1,128]{1,0:T(1,128)S(1)}) custom-call(s32[2]{0:T(128)S(1)} %pad_add_fusion.place, bf16[16,8,512]{2,1,0:T(8,128)(2,1)S(1)} %all-to-all-done.1.everyone, f32[5,4,128]{2,1,0:T(4,128)S(1)} %constant_dynamic-slice_fusion.truth, f32[1,512]{1,0:T(1,128)S(1)} %fusion.8.weight), custom_call_target="tpu_custom_call" | custom-call | tf_op jit(solution)/shard_map/pallas_call | solution.py:101
  49.4 0.0 copy-start.1
  49.4 0.7 copy-done.1
  50.1 4.5 %all-to-all-start.2 = ((bf16[16,16,512]{2,1,0:T(8,128)(2,1)}), bf16[16,16,512]{2,1,0:T(8,128)(2,1)S(1)}, u32[]{:S(2)}, u32[]{:S(2)}) async-start(bf16[16,16,512]{2,1,0:T(8,128)(2,1)} %copy-done.1), calls=%async_computation.2 | async-start | bytes 524288 | tf_op jit(solution)/shard_map/all_to_all | solution.py:42
  54.7 0.8 shard_map.146.slope
  55.4 8.2 %all-to-all-done.2.back = bf16[16,16,512]{2,1,0:T(8,128)(2,1)S(1)} async-done(((bf16[16,16,512]{2,1,0:T(8,128)(2,1)}), bf16[16,16,512]{2,1,0:T(8,128)(2,1)S(1)}, u32[]{:S(2)}, u32[]{:S(2)}) %all-to-all-start.2) | async-done | bytes 262176 | tf_op jit(solution)/shard_map/all_to_all | solution.py:42
  63.6 3.7 %shard_map.147 = (f32[32,24,128]{2,1,0:T(8,128)S(1)}, f32[32,24,128]{2,1,0:T(8,128)S(1)}) custom-call(s32[2]{0:T(128)S(1)} %pad_add_fusion.place, bf16[16,16,512]{2,1,0:T(8,128)(2,1)S(1)} %all-to-all-done.2.back, bf16[69,128]{1,0:T(8,128)(2,1)S(1)} %copy-done.2, bf16[512,128]{1,0:T(8,128)(2,1)S(1)} %get-tuple-element.34.residual, ...), custom_call_target="tpu_custom_call" | custom-call | tf_op jit(solution)/shard_map/pallas_call | solution.py:101
  67.4 1.9 %collective-permute-start.3 = (f32[32,24,128]{2,1,0:T(8,128)S(1)}, f32[32,24,128]{2,1,0:T(8,128)S(1)}, u32[]{:S(2)}, u32[]{:S(2)}) collective-permute-start(f32[32,24,128]{2,1,0:T(8,128)S(1)} %get-tuple-element.41), channel_id=1, source_target_pairs={{0,1},{1,0},{2,3},{3,2},{4,5},{5,4},{6,7},{7,6},{8,9},{9,8},{10,11... | collective-permute-start | bytes 1179656 | tf_op jit(solution)/shard_map/ppermute | solution.py:26
  69.3 1.7 %collective-permute-done.3 = f32[32,24,128]{2,1,0:T(8,128)S(1)} collective-permute-done((f32[32,24,128]{2,1,0:T(8,128)S(1)}, f32[32,24,128]{2,1,0:T(8,128)S(1)}, u32[]{:S(2)}, u32[]{:S(2)}) %collective-permute-start.3) | collective-permute-done | bytes 393248 | tf_op jit(solution)/shard_map/ppermute | solution.py:26
  71.0 22.3 %all_to_all.30 = bf16[32,24,128]{2,1,0:T(8,128)(2,1)S(1)} all-to-all(bf16[32,24,128]{2,1,0:T(8,128)(2,1)S(1)} %add_convert_fusion), channel_id=1, replica_groups={{0,16,32,48,64,80,96,112,128,144,160,176,192,208,224,240,256,272,288,30..., dimensions={0} | all-to-all | bytes 393216 | tf_op jit(solution)/shard_map/all_to_all | solution.py:42
  93.5 10.8 %all_to_all.31 = f32[8,10,128]{2,1,0:T(8,128)S(1)} all-to-all(f32[8,10,128]{2,1,0:T(8,128)S(1)} %pad_maximum_fusion.1), channel_id=1, replica_groups={{0,2,4,6,8,10,12,14},{1,3,5,7,9,11,13,15},{16,18,20,22,24,26,28,30},{17..., dimensions={0} | all-to-all | bytes 81920 | tf_op jit(solution)/shard_map/all_to_all | solution.py:42
  104.2 0.7 broadcast_in_dim.11
  104.9 4.8 %all-to-all-start.5 = ((f32[16,10,128]{2,1,0:T(8,128)}), f32[16,10,128]{2,1,0:T(8,128)S(1)}, u32[]{:S(2)}, u32[]{:S(2)}) async-start(f32[16,10,128]{2,1,0:T(8,128)} %broadcast_in_dim.11), calls=%async_computation.5 | async-start | bytes 262144 | tf_op jit(solution)/shard_map/all_to_all | solution.py:42
  109.7 0.2 shard_map.149
  109.8 0.7 reshape.102
  110.5 0.2 shard_map.150
  110.7 0.7 reshape.103
  111.4 5.6 %all-to-all-done.5.arrived = f32[16,10,128]{2,1,0:T(8,128)S(1)} async-done(((f32[16,10,128]{2,1,0:T(8,128)}), f32[16,10,128]{2,1,0:T(8,128)S(1)}, u32[]{:S(2)}, u32[]{:S(2)}) %all-to-all-start.5) | async-done | bytes 81952 | tf_op jit(solution)/shard_map/all_to_all | solution.py:42
  117.0 0.7 shard_map.148
  (12 shorter events, 0.2 us)
Async XLA Ops:
  0.6 39.8 %copy-start = (f32[69,4,128]{2,1,0:T(4,128)S(1)}, f32[69,4,128]{2,1,0:T(4,128)}, u32[]{:S(2)}) copy-start(f32[69,4,128]{2,1,0:T(4,128)} %param.10) | copy-start | bytes 423940
  0.6 0.8 copy-start.7
  2.1 13.4 %copy-start.5 = (bf16[4,128,128]{2,1,0:T(8,128)(2,1)S(1)}, bf16[4,128,128]{2,1,0:T(8,128)(2,1)}, u32[]{:S(2)}) copy-start(bf16[4,128,128]{2,1,0:T(8,128)(2,1)} %param.8) | copy-start | bytes 393220
  2.1 13.4 %copy-start.6 = (bf16[1,4,128,128]{3,2,1,0:T(8,128)(2,1)S(1)}, bf16[1,4,128,128]{3,2,1,0:T(8,128)(2,1)}, u32[]{:S(2)}) copy-start(bf16[1,4,128,128]{3,2,1,0:T(8,128)(2,1)} %param.9) | copy-start | bytes 393220
  2.1 24.1 %all-to-all-start = ((bf16[16,32,128]{2,1,0:T(8,128)(2,1)}), bf16[16,32,128]{2,1,0:T(8,128)(2,1)S(1)}, u32[]{:S(2)}, u32[]{:S(2)}) async-start(bf16[16,32,128]{2,1,0:T(8,128)(2,1)} %pad_maximum_fusion), calls=%async_computation | async-start | bytes 262144 | tf_op jit(solution)/shard_map/all_to_all | solution.py:42
  15.5 12.7 %copy-start.3 = (f32[49,128]{1,0:T(8,128)S(1)}, f32[49,128]{1,0:T(8,128)}, u32[]{:S(2)}) copy-start(f32[49,128]{1,0:T(8,128)} %taps.1) | copy-start | bytes 75268
  15.6 3.2 %collective-permute-start = (bf16[3,128,128]{2,1,0:T(8,128)(2,1)S(1)}, bf16[3,128,128]{2,1,0:T(8,128)(2,1)S(1)}, u32[]{:S(2)}, u32[]{:S(2)}) collective-permute-start(bf16[3,128,128]{2,1,0:T(8,128)(2,1)S(1)} %get-tuple-element.49), channel_id=1, source_target_pairs={{0,1},{1,0},{2,3},{3,2},{4,5},{5,4},{6,7},{7,6},{8,9},{9,8},{10,11... | collective-permute-start | bytes 294920 | tf_op jit(solution)/shard_map/ppermute | solution.py:26
  17.5 1.3 %collective-permute-start.1 = (bf16[3,128,128]{2,1,0:T(8,128)(2,1)S(1)}, bf16[3,128,128]{2,1,0:T(8,128)(2,1)S(1)}, u32[]{:S(2)}, u32[]{:S(2)}) collective-permute-start(bf16[3,128,128]{2,1,0:T(8,128)(2,1)S(1)} %get-tuple-element.48), channel_id=1, source_target_pairs={{1,2},{3,4},{5,6},{7,8},{9,10},{11,12},{13,14},{15,16},{17,18},{19... | collective-permute-start | bytes 294920 | tf_op jit(solution)/shard_map/ppermute | solution.py:32
  26.2 4.7 %collective-permute-start.2 = (bf16[16,32,128]{2,1,0:T(8,128)(2,1)S(1)}, bf16[16,32,128]{2,1,0:T(8,128)(2,1)S(1)}, u32[]{:S(2)}, u32[]{:S(2)}) collective-permute-start(bf16[16,32,128]{2,1,0:T(8,128)(2,1)S(1)} %all-to-all-done.mine), channel_id=1, source_target_pairs={{0,1},{1,0},{2,3},{3,2},{4,5},{5,4},{6,7},{7,6},{8,9},{9,8},{10,11... | collective-permute-start | bytes 393224 | tf_op jit(solution)/shard_map/ppermute | solution.py:26
  28.2 0.7 copy-start.4
  28.9 2.0 %copy-start.2 = (bf16[69,128]{1,0:T(8,128)(2,1)S(1)}, bf16[69,128]{1,0:T(8,128)(2,1)}, u32[]{:S(2)}) copy-start(bf16[69,128]{1,0:T(8,128)(2,1)} %readout.5) | copy-start | bytes 52996
  32.8 15.1 %all-to-all-start.1 = ((bf16[16,8,512]{2,1,0:T(8,128)(2,1)}), bf16[16,8,512]{2,1,0:T(8,128)(2,1)S(1)}, u32[]{:S(2)}, u32[]{:S(2)}) async-start(bf16[16,8,512]{2,1,0:T(8,128)(2,1)} %get-tuple-element.32), calls=%async_computation.1 | async-start | bytes 262144 | tf_op jit(solution)/shard_map/all_to_all | solution.py:42
  49.4 0.7 copy-start.1
  50.1 13.5 %all-to-all-start.2 = ((bf16[16,16,512]{2,1,0:T(8,128)(2,1)}), bf16[16,16,512]{2,1,0:T(8,128)(2,1)S(1)}, u32[]{:S(2)}, u32[]{:S(2)}) async-start(bf16[16,16,512]{2,1,0:T(8,128)(2,1)} %copy-done.1), calls=%async_computation.2 | async-start | bytes 524288 | tf_op jit(solution)/shard_map/all_to_all | solution.py:42
  67.4 3.6 %collective-permute-start.3 = (f32[32,24,128]{2,1,0:T(8,128)S(1)}, f32[32,24,128]{2,1,0:T(8,128)S(1)}, u32[]{:S(2)}, u32[]{:S(2)}) collective-permute-start(f32[32,24,128]{2,1,0:T(8,128)S(1)} %get-tuple-element.41), channel_id=1, source_target_pairs={{0,1},{1,0},{2,3},{3,2},{4,5},{5,4},{6,7},{7,6},{8,9},{9,8},{10,11... | collective-permute-start | bytes 1179656 | tf_op jit(solution)/shard_map/ppermute | solution.py:26
  104.9 12.1 %all-to-all-start.5 = ((f32[16,10,128]{2,1,0:T(8,128)}), f32[16,10,128]{2,1,0:T(8,128)S(1)}, u32[]{:S(2)}, u32[]{:S(2)}) async-start(f32[16,10,128]{2,1,0:T(8,128)} %broadcast_in_dim.11), calls=%async_computation.5 | async-start | bytes 262144 | tf_op jit(solution)/shard_map/all_to_all | solution.py:42

commit v2 on v1

--- a/solution.py
+++ b/solution.py
@@ -294,7 +294,7 @@
     back_depth[...] = inverse[...] * (g - p - value * q)
 
 
-def pack_body(back_depth, ext, widen_grad, shrink_grad, readout_grad, gain_grad, loss, send, keep, small):
+def pack_body(back_depth, ext, widen_grad, shrink_grad, readout_grad, gain_grad, loss, packet, small, core):
     half = STENCIL_SIDE // 2
     zonal = ext.shape[1] - 2 * EDGE
     rows = back_depth.shape[0] // zonal
@@ -326,18 +326,20 @@
         for h in range(2):
             d = 2 * e + h
             for mat, grad in enumerate((widen_grad, shrink_grad)):
-                at = slice(mat * depth_z, (mat + 1) * depth_z)
                 base = h * depth_z * members + e
-                keep[d, at, :] = grad[pl.ds(base, depth_z, stride=members), :]
+                ours = grad[pl.ds(base, depth_z, stride=members), :]
                 base = base + 2 * depth_z * members
-                send[d, at, :] = grad[pl.ds(base, depth_z, stride=members), :]
-            keep[d, 2 * depth_z :, :] = tail
-            send[d, 2 * depth_z :, :] = tail
+                others = grad[pl.ds(base, depth_z, stride=members), :]
+                first = jnp.where(core == 0, ours, others)
+                second = jnp.where(core == 0, others, ours)
+                at = slice(2 * mat * depth_z, 2 * (mat + 1) * depth_z)
+                packet[d, at, :] = jnp.concatenate([first, second], axis=0).astype(BF16)
+            packet[d, 4 * depth_z :, :] = tail.astype(BF16)
 
 
 def gradient_body(
     place, back, readout, residual, gated, slope, normed, scaled, inverse, gain, mine, theirs, loss,
-    field, partner, other, send, keep, ext, gate, back_upper, widen_grad, shrink_grad, readout_grad, gain_grad, back_depth, small,
+    field, partner, other, packet, ext, gate, back_upper, widen_grad, shrink_grad, readout_grad, gain_grad, back_depth, small,
 ):
     fill_rows(place, field, partner, other, ext)
     backward_body(
@@ -346,7 +348,7 @@
     )
     pack_body(
         back_depth, ext, widen_grad, shrink_grad, readout_grad, gain_grad, loss,
-        send, keep, small,
+        packet, small, place[0],
     )
 
 
@@ -440,10 +442,9 @@
     (average,) = vmem_call(average_body, [((variables, points), F32)], vectors=1)(back)
     sample_average_spread = average.reshape(1, variables, rows, zonal)
 
-    packet = ((2 * members, 2 * depth_z + share, channels), F32)
-    send, keep = vmem_call(
+    (packet,) = vmem_call(
         gradient_body,
-        [packet, packet],
+        [((2 * members, 4 * depth_z + share, channels), BF16)],
         [
             pltpu.VMEM(wide, F32),
             pltpu.VMEM((points, hidden), F32),
@@ -462,19 +463,18 @@
         theirs, loss, field, partner, other,
     )
 
-    total = (keep + core_swap(send)).astype(BF16)
-    arrived = exchange(total, AXES, plane_groups(members, bands)).astype(F32)
-    columns = [
-        list(range(h * bands // 2 + c, (h + 1) * bands // 2, 2)) for h in range(2) for c in range(2)
-    ]
+    arrived = exchange(packet, AXES, plane_groups(members, bands)).astype(F32)
     part = jnp.sum(arrived, axis=0)
     outgoing = jnp.concatenate(
         [
-            jnp.broadcast_to(part[None, 2 * depth_z :], (depth_z, share, channels)),
-            part[: 2 * depth_z].reshape(2, depth_z, channels).transpose(1, 0, 2),
+            jnp.broadcast_to(part[None, 4 * depth_z :], (2 * depth_z, share, channels)),
+            part[: 4 * depth_z].reshape(2, 2, depth_z, channels).transpose(2, 1, 0, 3).reshape(
+                2 * depth_z, 2, channels
+            ),
         ],
         axis=1,
     )
+    columns = [list(range(h * bands // 2, (h + 1) * bands // 2)) for h in range(2)]
     done = jnp.sum(exchange(outgoing, "lat", columns), axis=0)
     arrived = exchange(jnp.broadcast_to(done[None], (members,) + done.shape), "ens")
     up, down, taps, gain_total, readout, loss = vmem_call(

time: 118 us -> 119 us (level)
  the two profiles are of different devices: /device:TPU:8 before, /device:TPU:1 now
where the time goes in v2:
time: 119 us
  starting transfers between devices  38.6 us (32%)
  blocking collectives  36.3 us (31%)
  waiting for transfers between devices  25.4 us (21%)
  Pallas kernels  11.6 us (10%)
  local copies, waits for them, and re-layouts  4.79 us (4%)
    all_to_all x2, blocking collectives, exchange(): lax.all_to_all(value, axis, 0, 0, tiled=True, axis_index_groups=groups)  36.3 us
    all_to_all x4, starting transfers between devices, exchange(): lax.all_to_all(value, axis, 0, 0, tiled=True, axis_index_groups=groups)  28.3 us
    all_to_all x4, waiting for transfers between devices, exchange(): lax.all_to_all(value, axis, 0, 0, tiled=True, axis_index_groups=groups)  22.3 us
    pallas_call x8, Pallas kernels, run(): return call(*operands)  11.6 us
    ppermute x2, starting transfers between devices, core_swap(): return lax.ppermute(value, 'lat', [(i, i ^ 1) for i in range(count)])  6.94 us
    ppermute x1, starting transfers between devices, odd_swap(): return lax.ppermute(value, 'lat', pairs + [(b, a) for a, b in pairs])  3.44 us
    ppermute x1, waiting for transfers between devices, odd_swap(): return lax.ppermute(value, 'lat', pairs + [(b, a) for a, b in pairs])  3.11 us
  transfers between devices with their start and end apart: 7, of which 4 were waited for; matrix products, arithmetic and copies ran while one was open for 1% of the time, Pallas kernels for 3%

profile of v2, /device:TPU:1, one launch (start us, length us, event | category | flops | bytes accessed | tf_op | source)
XLA Modules:
  0.0 118.6 jit_solution(6810209340368114265)
XLA Ops:
  0.6 0.0 copy-start
  0.6 0.0 copy-start.7
  0.7 0.7 broadcast_in_dim.8
  1.4 0.0 copy-done.7
  1.4 0.7 pad_maximum_fusion
  2.1 0.0 copy-start.4
  2.1 0.0 copy-start.5
  2.1 14.8 %all-to-all-start = ((bf16[16,32,128]{2,1,0:T(8,128)(2,1)}), bf16[16,32,128]{2,1,0:T(8,128)(2,1)S(1)}, u32[]{:S(2)}, u32[]{:S(2)}) async-start(bf16[16,32,128]{2,1,0:T(8,128)(2,1)} %pad_maximum_fusion), calls=%async_computation | async-start | bytes 262144 | tf_op jit(solution)/shard_map/all_to_all | solution.py:42
  16.9 0.0 copy-done.4
  16.9 0.0 copy-done.5
  17.0 0.0 copy-start.2
  17.0 2.9 %collective-permute-start = (bf16[3,128,128]{2,1,0:T(8,128)(2,1)S(1)}, bf16[3,128,128]{2,1,0:T(8,128)(2,1)S(1)}, u32[]{:S(2)}, u32[]{:S(2)}) collective-permute-start(bf16[3,128,128]{2,1,0:T(8,128)(2,1)S(1)} %get-tuple-element.45), channel_id=1, source_target_pairs={{0,1},{1,0},{2,3},{3,2},{4,5},{5,4},{6,7},{7,6},{8,9},{9,8},{10,11... | collective-permute-start | bytes 294920 | tf_op jit(solution)/shard_map/ppermute | solution.py:26
  19.9 3.4 %collective-permute-start.1 = (bf16[3,128,128]{2,1,0:T(8,128)(2,1)S(1)}, bf16[3,128,128]{2,1,0:T(8,128)(2,1)S(1)}, u32[]{:S(2)}, u32[]{:S(2)}) collective-permute-start(bf16[3,128,128]{2,1,0:T(8,128)(2,1)S(1)} %get-tuple-element.44), channel_id=1, source_target_pairs={{1,2},{3,4},{5,6},{7,8},{9,10},{11,12},{13,14},{15,16},{17,18},{19... | collective-permute-start | bytes 294920 | tf_op jit(solution)/shard_map/ppermute | solution.py:32
  23.3 0.0 collective-permute-done.partner
  23.3 3.1 %collective-permute-done.1.other = bf16[3,128,128]{2,1,0:T(8,128)(2,1)S(1)} collective-permute-done((bf16[3,128,128]{2,1,0:T(8,128)(2,1)S(1)}, bf16[3,128,128]{2,1,0:T(8,128)(2,1)S(1)}, u32[]{:S(2)}, u32[]{:S(2)}) %collective-permute-start.1) | collective-permute-done | bytes 98336 | tf_op jit(solution)/shard_map/ppermute | solution.py:32
  26.4 0.0 all-to-all-done.mine
  26.4 4.1 %collective-permute-start.2 = (bf16[16,32,128]{2,1,0:T(8,128)(2,1)S(1)}, bf16[16,32,128]{2,1,0:T(8,128)(2,1)S(1)}, u32[]{:S(2)}, u32[]{:S(2)}) collective-permute-start(bf16[16,32,128]{2,1,0:T(8,128)(2,1)S(1)} %all-to-all-done.mine), channel_id=1, source_target_pairs={{0,1},{1,0},{2,3},{3,2},{4,5},{5,4},{6,7},{7,6},{8,9},{9,8},{10,11... | collective-permute-start | bytes 393224 | tf_op jit(solution)/shard_map/ppermute | solution.py:26
  30.5 0.1 pad_add_fusion.place
  30.6 0.0 copy-start.3
  30.6 0.0 copy-done.2
  30.6 0.7 copy-done.3
  31.3 0.0 copy-start.1
  31.3 2.0 %shard_map.143 = (f32[512,128]{1,0:T(8,128)S(1)}, f32[512,128]{1,0:T(8,128)S(1)}, bf16[512,128]{1,0:T(8,128)(2,1)S(1)}) custom-call(s32[2]{0:T(128)S(1)} %pad_add_fusion.place, bf16[4,128,128]{2,1,0:T(8,128)(2,1)S(1)} %fusion.field, bf16[3,128,128]{2,1,0:T(8,128)(2,1)S(1)} %collective-permute-done.partner, ...), custom_call_target="tpu_custom_call" | custom-call | tf_op jit(solution)/shard_map/pallas_call | solution.py:101
  33.3 0.0 collective-permute-done.2.theirs
  33.3 0.0 copy-done.1
  33.3 1.9 %shard_map.144 = (bf16[512,512]{1,0:T(8,128)(2,1)S(1)}, f32[512,512]{1,0:T(8,128)S(1)}, bf16[512,128]{1,0:T(8,128)(2,1)S(1)}, bf16[16,8,512]{2,1,0:T(8,128)(2,1)}) custom-call(bf16[512,128]{1,0:T(8,128)(2,1)S(1)} %get-tuple-element.28.normed, bf16[16,32,128]{2,1,0:T(8,128)(2,1)S(1)} %all-to-all-done.mine, ...), custom_call_target="tpu_custom_call" | custom-call | tf_op jit(solution)/shard_map/pallas_call | solution.py:101
  35.2 6.0 %all-to-all-start.1 = ((bf16[16,8,512]{2,1,0:T(8,128)(2,1)}), bf16[16,8,512]{2,1,0:T(8,128)(2,1)S(1)}, u32[]{:S(2)}, u32[]{:S(2)}) async-start(bf16[16,8,512]{2,1,0:T(8,128)(2,1)} %get-tuple-element.30), calls=%async_computation.1 | async-start | bytes 262144 | tf_op jit(solution)/shard_map/all_to_all | solution.py:42
  41.3 0.1 fusion.8.weight
  41.3 0.0 copy-done
  41.4 7.1 %all-to-all-done.1.everyone = bf16[16,8,512]{2,1,0:T(8,128)(2,1)S(1)} async-done(((bf16[16,8,512]{2,1,0:T(8,128)(2,1)}), bf16[16,8,512]{2,1,0:T(8,128)(2,1)S(1)}, u32[]{:S(2)}, u32[]{:S(2)}) %all-to-all-start.1) | async-done | bytes 131104 | tf_op jit(solution)/shard_map/all_to_all | solution.py:42
  48.5 2.2 %shard_map.145 = (bf16[16,16,512]{2,1,0:T(8,128)(2,1)}, f32[1,128]{1,0:T(1,128)S(1)}) custom-call(s32[2]{0:T(128)S(1)} %pad_add_fusion.place, bf16[16,8,512]{2,1,0:T(8,128)(2,1)S(1)} %all-to-all-done.1.everyone, f32[5,4,128]{2,1,0:T(4,128)S(1)} %constant_dynamic-slice_fusion.truth, f32[1,512]{1,0:T(1,128)S(1)} %fusion.8.weight), custom_call_target="tpu_custom_call" | custom-call | tf_op jit(solution)/shard_map/pallas_call | solution.py:101
  50.7 4.0 %all-to-all-start.2 = ((bf16[16,16,512]{2,1,0:T(8,128)(2,1)}), bf16[16,16,512]{2,1,0:T(8,128)(2,1)S(1)}, u32[]{:S(2)}, u32[]{:S(2)}) async-start(bf16[16,16,512]{2,1,0:T(8,128)(2,1)} %get-tuple-element.31), calls=%async_computation.2 | async-start | bytes 524288 | tf_op jit(solution)/shard_map/all_to_all | solution.py:42
  54.6 0.8 shard_map.146.slope
  55.4 9.1 %all-to-all-done.2.back = bf16[16,16,512]{2,1,0:T(8,128)(2,1)S(1)} async-done(((bf16[16,16,512]{2,1,0:T(8,128)(2,1)}), bf16[16,16,512]{2,1,0:T(8,128)(2,1)S(1)}, u32[]{:S(2)}, u32[]{:S(2)}) %all-to-all-start.2) | async-done | bytes 262176 | tf_op jit(solution)/shard_map/all_to_all | solution.py:42
  64.5 3.8 %shard_map.147 = bf16[32,40,128]{2,1,0:T(8,128)(2,1)S(1)} custom-call(s32[2]{0:T(128)S(1)} %pad_add_fusion.place, bf16[16,16,512]{2,1,0:T(8,128)(2,1)S(1)} %all-to-all-done.2.back, bf16[69,128]{1,0:T(8,128)(2,1)S(1)} %copy-done.1, bf16[512,128]{1,0:T(8,128)(2,1)S(1)} %get-tuple-element.32.residual, bf16[512,512]{1,0:T(8,128)(2,1)S(1)} %get-tuple-element.33.gated, ...), custom_call_target="tpu_custom_call" | custom-call | tf_op jit(solution)/shard_map/pallas_call | solution.py:101
  68.3 20.2 %all_to_all.30 = bf16[32,40,128]{2,1,0:T(8,128)(2,1)S(1)} all-to-all(bf16[32,40,128]{2,1,0:T(8,128)(2,1)S(1)} %shard_map.147), channel_id=1, replica_groups={{0,16,32,48,64,80,96,112,128,144,160,176,192,208,224,240,256,272,288,30..., dimensions={0} | all-to-all | bytes 655360 | tf_op jit(solution)/shard_map/all_to_all | solution.py:42
  88.5 0.1 convert_reduce_fusion
  88.5 0.0 copy-start.6
  88.6 0.6 copy-done.6
  89.2 0.0 slice-start
  89.2 0.7 slice-done
  89.9 16.2 %all_to_all.31 = f32[16,10,128]{2,1,0:T(8,128)S(1)} all-to-all(f32[16,10,128]{2,1,0:T(8,128)S(1)} %pad_maximum_fusion.1), channel_id=1, replica_groups={{0,1,2,3,4,5,6,7,8,9,10,11,12,13,14,15},{16,17,18,19,20,21,22,23,24,25,..., dimensions={0} | all-to-all | bytes 163840 | tf_op jit(solution)/shard_map/all_to_all | solution.py:42
  106.0 0.7 broadcast_in_dim.11
  106.7 3.5 %all-to-all-start.5 = ((f32[16,10,128]{2,1,0:T(8,128)}), f32[16,10,128]{2,1,0:T(8,128)S(1)}, u32[]{:S(2)}, u32[]{:S(2)}) async-start(f32[16,10,128]{2,1,0:T(8,128)} %broadcast_in_dim.11), calls=%async_computation.5 | async-start | bytes 262144 | tf_op jit(solution)/shard_map/all_to_all | solution.py:42
  110.2 0.2 shard_map.149
  110.4 0.7 reshape.106
  111.1 0.2 shard_map.150
  111.2 0.7 reshape.107
  112.0 6.0 %all-to-all-done.5.arrived = f32[16,10,128]{2,1,0:T(8,128)S(1)} async-done(((f32[16,10,128]{2,1,0:T(8,128)}), f32[16,10,128]{2,1,0:T(8,128)S(1)}, u32[]{:S(2)}, u32[]{:S(2)}) %all-to-all-start.5) | async-done | bytes 81952 | tf_op jit(solution)/shard_map/all_to_all | solution.py:42
  118.0 0.7 shard_map.148
  (10 shorter events, 0.1 us)
Async XLA Ops:
  0.6 40.7 %copy-start = (f32[69,4,128]{2,1,0:T(4,128)S(1)}, f32[69,4,128]{2,1,0:T(4,128)}, u32[]{:S(2)}) copy-start(f32[69,4,128]{2,1,0:T(4,128)} %param.10) | copy-start | bytes 423940
  0.6 0.8 copy-start.7
  2.1 14.8 %copy-start.4 = (bf16[4,128,128]{2,1,0:T(8,128)(2,1)S(1)}, bf16[4,128,128]{2,1,0:T(8,128)(2,1)}, u32[]{:S(2)}) copy-start(bf16[4,128,128]{2,1,0:T(8,128)(2,1)} %param.8) | copy-start | bytes 393220
  2.1 14.8 %copy-start.5 = (bf16[1,4,128,128]{3,2,1,0:T(8,128)(2,1)S(1)}, bf16[1,4,128,128]{3,2,1,0:T(8,128)(2,1)}, u32[]{:S(2)}) copy-start(bf16[1,4,128,128]{3,2,1,0:T(8,128)(2,1)} %param.9) | copy-start | bytes 393220
  2.1 24.3 %all-to-all-start = ((bf16[16,32,128]{2,1,0:T(8,128)(2,1)}), bf16[16,32,128]{2,1,0:T(8,128)(2,1)S(1)}, u32[]{:S(2)}, u32[]{:S(2)}) async-start(bf16[16,32,128]{2,1,0:T(8,128)(2,1)} %pad_maximum_fusion), calls=%async_computation | async-start | bytes 262144 | tf_op jit(solution)/shard_map/all_to_all | solution.py:42
  17.0 13.6 %copy-start.2 = (f32[49,128]{1,0:T(8,128)S(1)}, f32[49,128]{1,0:T(8,128)}, u32[]{:S(2)}) copy-start(f32[49,128]{1,0:T(8,128)} %taps.1) | copy-start | bytes 75268
  17.0 6.3 %collective-permute-start = (bf16[3,128,128]{2,1,0:T(8,128)(2,1)S(1)}, bf16[3,128,128]{2,1,0:T(8,128)(2,1)S(1)}, u32[]{:S(2)}, u32[]{:S(2)}) collective-permute-start(bf16[3,128,128]{2,1,0:T(8,128)(2,1)S(1)} %get-tuple-element.45), channel_id=1, source_target_pairs={{0,1},{1,0},{2,3},{3,2},{4,5},{5,4},{6,7},{7,6},{8,9},{9,8},{10,11... | collective-permute-start | bytes 294920 | tf_op jit(solution)/shard_map/ppermute | solution.py:26
  19.9 6.6 %collective-permute-start.1 = (bf16[3,128,128]{2,1,0:T(8,128)(2,1)S(1)}, bf16[3,128,128]{2,1,0:T(8,128)(2,1)S(1)}, u32[]{:S(2)}, u32[]{:S(2)}) collective-permute-start(bf16[3,128,128]{2,1,0:T(8,128)(2,1)S(1)} %get-tuple-element.44), channel_id=1, source_target_pairs={{1,2},{3,4},{5,6},{7,8},{9,10},{11,12},{13,14},{15,16},{17,18},{19... | collective-permute-start | bytes 294920 | tf_op jit(solution)/shard_map/ppermute | solution.py:32
  26.4 6.8 %collective-permute-start.2 = (bf16[16,32,128]{2,1,0:T(8,128)(2,1)S(1)}, bf16[16,32,128]{2,1,0:T(8,128)(2,1)S(1)}, u32[]{:S(2)}, u32[]{:S(2)}) collective-permute-start(bf16[16,32,128]{2,1,0:T(8,128)(2,1)S(1)} %all-to-all-done.mine), channel_id=1, source_target_pairs={{0,1},{1,0},{2,3},{3,2},{4,5},{5,4},{6,7},{7,6},{8,9},{9,8},{10,11... | collective-permute-start | bytes 393224 | tf_op jit(solution)/shard_map/ppermute | solution.py:26
  30.6 0.7 copy-start.3
  31.3 2.0 %copy-start.1 = (bf16[69,128]{1,0:T(8,128)(2,1)S(1)}, bf16[69,128]{1,0:T(8,128)(2,1)}, u32[]{:S(2)}) copy-start(bf16[69,128]{1,0:T(8,128)(2,1)} %readout.5) | copy-start | bytes 52996
  35.2 13.3 %all-to-all-start.1 = ((bf16[16,8,512]{2,1,0:T(8,128)(2,1)}), bf16[16,8,512]{2,1,0:T(8,128)(2,1)S(1)}, u32[]{:S(2)}, u32[]{:S(2)}) async-start(bf16[16,8,512]{2,1,0:T(8,128)(2,1)} %get-tuple-element.30), calls=%async_computation.1 | async-start | bytes 262144 | tf_op jit(solution)/shard_map/all_to_all | solution.py:42
  50.7 13.9 %all-to-all-start.2 = ((bf16[16,16,512]{2,1,0:T(8,128)(2,1)}), bf16[16,16,512]{2,1,0:T(8,128)(2,1)S(1)}, u32[]{:S(2)}, u32[]{:S(2)}) async-start(bf16[16,16,512]{2,1,0:T(8,128)(2,1)} %get-tuple-element.31), calls=%async_computation.2 | async-start | bytes 524288 | tf_op jit(solution)/shard_map/all_to_all | solution.py:42
  88.5 0.6 copy-start.6
  89.2 0.7 slice-start
  106.7 11.3 %all-to-all-start.5 = ((f32[16,10,128]{2,1,0:T(8,128)}), f32[16,10,128]{2,1,0:T(8,128)S(1)}, u32[]{:S(2)}, u32[]{:S(2)}) async-start(f32[16,10,128]{2,1,0:T(8,128)} %broadcast_in_dim.11), calls=%async_computation.5 | async-start | bytes 262144 | tf_op jit(solution)/shard_map/all_to_all | solution.py:42

commit v3 on v1

--- a/solution.py
+++ b/solution.py
@@ -139,7 +139,7 @@
         centred = total - jnp.mean(total, axis=-1, keepdims=True)
         recip = lax.rsqrt(jnp.mean(centred * centred, axis=-1, keepdims=True) + EPSILON)
         value = centred * recip
-        rounded = (gain[...][None] * value).astype(BF16)
+        rounded = (gain[0:1, :][None] * value).astype(BF16)
         wide = jnp.broadcast_to(recip, value.shape)
         for i in range(rows):
             at = pl.ds(i * zonal + start, STRIP)
@@ -288,7 +288,7 @@
     value = scaled[...]
     product = back_norm * value
     gain_grad[...] = jnp.sum(product, axis=0, keepdims=True)
-    g = back_norm * gain[...]
+    g = back_norm * gain[0:1, :]
     p = jnp.mean(g, axis=-1, keepdims=True)
     q = jnp.mean(g * value, axis=-1, keepdims=True)
     back_depth[...] = inverse[...] * (g - p - value * q)
@@ -383,7 +383,7 @@
     depth_z = DEPTH_Z
     share = CHUNK_ROWS
     place = jnp.stack([lax.rem(band, 2), member]).astype(jnp.int32)
-    gain = affine_factor.reshape(1, channels)
+    gain = lax.optimization_barrier(jnp.broadcast_to(affine_factor[None], (8, channels)))
 
     field = (features.astype(F32) + random_perturbation[0].astype(F32)).astype(BF16)
     partner, other = halo_rows(field, half)

time: 118 us -> 118 us (level)
  no operation moved by 1% of the time
where the time goes in v3:
time: 118 us
  starting transfers between devices  36.6 us (31%)
  blocking collectives  33.1 us (28%)
  waiting for transfers between devices  31 us (26%)
  Pallas kernels  11.6 us (10%)
  local copies, waits for them, and re-layouts  3.54 us (3%)
    all_to_all x2, blocking collectives, exchange(): lax.all_to_all(value, axis, 0, 0, tiled=True, axis_index_groups=groups)  33.1 us
    all_to_all x4, starting transfers between devices, exchange(): lax.all_to_all(value, axis, 0, 0, tiled=True, axis_index_groups=groups)  30.2 us
    all_to_all x4, waiting for transfers between devices, exchange(): lax.all_to_all(value, axis, 0, 0, tiled=True, axis_index_groups=groups)  28.7 us
    pallas_call x8, Pallas kernels, run(): return call(*operands)  11.6 us
    ppermute x3, starting transfers between devices, core_swap(): return lax.ppermute(value, 'lat', [(i, i ^ 1) for i in range(count)])  5.75 us
  transfers between devices with their start and end apart: 8, of which 6 were waited for; matrix products, arithmetic and copies ran while one was open for 1% of the time, Pallas kernels for 3%

profile of v3, /device:TPU:8, one launch (start us, length us, event | category | flops | bytes accessed | tf_op | source)
XLA Modules:
  0.0 117.7 jit_solution(6463808212846627073)
XLA Ops:
  0.6 0.0 copy-start
  0.6 0.0 copy-start.5
  0.7 0.7 broadcast_in_dim.10
  1.4 0.0 copy-done.5
  1.4 0.7 pad_maximum_fusion
  2.1 0.0 copy-start.3
  2.1 0.0 copy-start.4
  2.1 13.3 %all-to-all-start = ((bf16[16,32,128]{2,1,0:T(8,128)(2,1)}), bf16[16,32,128]{2,1,0:T(8,128)(2,1)S(1)}, u32[]{:S(2)}, u32[]{:S(2)}) async-start(bf16[16,32,128]{2,1,0:T(8,128)(2,1)} %pad_maximum_fusion), calls=%async_computation | async-start | bytes 262144 | tf_op jit(solution)/shard_map/all_to_all | solution.py:42
  15.5 0.0 copy-done.3
  15.5 0.0 copy-done.4
  15.5 0.0 copy-start.2
  15.6 1.9 %collective-permute-start = (bf16[3,128,128]{2,1,0:T(8,128)(2,1)S(1)}, bf16[3,128,128]{2,1,0:T(8,128)(2,1)S(1)}, u32[]{:S(2)}, u32[]{:S(2)}) collective-permute-start(bf16[3,128,128]{2,1,0:T(8,128)(2,1)S(1)} %get-tuple-element.49), channel_id=1, source_target_pairs={{0,1},{1,0},{2,3},{3,2},{4,5},{5,4},{6,7},{7,6},{8,9},{9,8},{10,11... | collective-permute-start | bytes 294920 | tf_op jit(solution)/shard_map/ppermute | solution.py:26
  17.5 0.7 collective-permute-start.1
  18.2 0.6 collective-permute-done.partner
  18.8 0.0 collective-permute-done.1.other
  18.8 7.4 %all-to-all-done.mine = bf16[16,32,128]{2,1,0:T(8,128)(2,1)S(1)} async-done(((bf16[16,32,128]{2,1,0:T(8,128)(2,1)}), bf16[16,32,128]{2,1,0:T(8,128)(2,1)S(1)}, u32[]{:S(2)}, u32[]{:S(2)}) %all-to-all-start) | async-done | bytes 131104 | tf_op jit(solution)/shard_map/all_to_all | solution.py:42
  26.2 1.9 %collective-permute-start.2 = (bf16[16,32,128]{2,1,0:T(8,128)(2,1)S(1)}, bf16[16,32,128]{2,1,0:T(8,128)(2,1)S(1)}, u32[]{:S(2)}, u32[]{:S(2)}) collective-permute-start(bf16[16,32,128]{2,1,0:T(8,128)(2,1)S(1)} %all-to-all-done.mine), channel_id=1, source_target_pairs={{0,1},{1,0},{2,3},{3,2},{4,5},{5,4},{6,7},{7,6},{8,9},{9,8},{10,11... | collective-permute-start | bytes 393224 | tf_op jit(solution)/shard_map/ppermute | solution.py:26
  28.1 0.0 copy-start.6
  28.1 0.6 copy-done.6
  28.8 0.1 pad_add_fusion.place
  28.9 0.0 copy-done.2
  28.9 0.0 copy-start.1
  28.9 2.0 %shard_map.143 = (f32[512,128]{1,0:T(8,128)S(1)}, f32[512,128]{1,0:T(8,128)S(1)}, bf16[512,128]{1,0:T(8,128)(2,1)S(1)}) custom-call(s32[2]{0:T(128)S(1)} %pad_add_fusion.place, bf16[4,128,128]{2,1,0:T(8,128)(2,1)S(1)} %fusion.field, bf16[3,128,128]{2,1,0:T(8,128)(2,1)S(1)} %collective-permute-done.partner, ...), custom_call_target="tpu_custom_call" | custom-call | tf_op jit(solution)/shard_map/pallas_call | solution.py:101
  30.9 0.0 collective-permute-done.2.theirs
  30.9 0.0 copy-done.1
  30.9 1.9 %shard_map.144 = (bf16[512,512]{1,0:T(8,128)(2,1)S(1)}, f32[512,512]{1,0:T(8,128)S(1)}, bf16[512,128]{1,0:T(8,128)(2,1)S(1)}, bf16[16,8,512]{2,1,0:T(8,128)(2,1)}) custom-call(bf16[512,128]{1,0:T(8,128)(2,1)S(1)} %get-tuple-element.30.normed, bf16[16,32,128]{2,1,0:T(8,128)(2,1)S(1)} %all-to-all-done.mine, ...), custom_call_target="tpu_custom_call" | custom-call | tf_op jit(solution)/shard_map/pallas_call | solution.py:101
  32.8 7.6 %all-to-all-start.1 = ((bf16[16,8,512]{2,1,0:T(8,128)(2,1)}), bf16[16,8,512]{2,1,0:T(8,128)(2,1)S(1)}, u32[]{:S(2)}, u32[]{:S(2)}) async-start(bf16[16,8,512]{2,1,0:T(8,128)(2,1)} %get-tuple-element.32), calls=%async_computation.1 | async-start | bytes 262144 | tf_op jit(solution)/shard_map/all_to_all | solution.py:42
  40.4 0.1 fusion.8.weight
  40.5 0.0 copy-done
  40.5 7.5 %all-to-all-done.1.everyone = bf16[16,8,512]{2,1,0:T(8,128)(2,1)S(1)} async-done(((bf16[16,8,512]{2,1,0:T(8,128)(2,1)}), bf16[16,8,512]{2,1,0:T(8,128)(2,1)S(1)}, u32[]{:S(2)}, u32[]{:S(2)}) %all-to-all-start.1) | async-done | bytes 131104 | tf_op jit(solution)/shard_map/all_to_all | solution.py:42
  48.0 2.1 %shard_map.145 = (bf16[16,16,512]{2,1,0:T(8,128)(2,1)}, f32[1,128]{1,0:T(1,128)S(1)}) custom-call(s32[2]{0:T(128)S(1)} %pad_add_fusion.place, bf16[16,8,512]{2,1,0:T(8,128)(2,1)S(1)} %all-to-all-done.1.everyone, f32[5,4,128]{2,1,0:T(4,128)S(1)} %constant_dynamic-slice_fusion.truth, f32[1,512]{1,0:T(1,128)S(1)} %fusion.8.weight), custom_call_target="tpu_custom_call" | custom-call | tf_op jit(solution)/shard_map/pallas_call | solution.py:101
  50.1 4.5 %all-to-all-start.2 = ((bf16[16,16,512]{2,1,0:T(8,128)(2,1)}), bf16[16,16,512]{2,1,0:T(8,128)(2,1)S(1)}, u32[]{:S(2)}, u32[]{:S(2)}) async-start(bf16[16,16,512]{2,1,0:T(8,128)(2,1)} %get-tuple-element.33), calls=%async_computation.2 | async-start | bytes 524288 | tf_op jit(solution)/shard_map/all_to_all | solution.py:42
  54.7 0.8 shard_map.146.slope
  55.4 8.2 %all-to-all-done.2.back = bf16[16,16,512]{2,1,0:T(8,128)(2,1)S(1)} async-done(((bf16[16,16,512]{2,1,0:T(8,128)(2,1)}), bf16[16,16,512]{2,1,0:T(8,128)(2,1)S(1)}, u32[]{:S(2)}, u32[]{:S(2)}) %all-to-all-start.2) | async-done | bytes 262176 | tf_op jit(solution)/shard_map/all_to_all | solution.py:42
  63.6 3.7 %shard_map.147 = (f32[32,24,128]{2,1,0:T(8,128)S(1)}, f32[32,24,128]{2,1,0:T(8,128)S(1)}) custom-call(s32[2]{0:T(128)S(1)} %pad_add_fusion.place, bf16[16,16,512]{2,1,0:T(8,128)(2,1)S(1)} %all-to-all-done.2.back, bf16[69,128]{1,0:T(8,128)(2,1)S(1)} %copy-done.1, bf16[512,128]{1,0:T(8,128)(2,1)S(1)} %get-tuple-element.34.residual, ...), custom_call_target="tpu_custom_call" | custom-call | tf_op jit(solution)/shard_map/pallas_call | solution.py:101
  67.4 1.9 %collective-permute-start.3 = (f32[32,24,128]{2,1,0:T(8,128)S(1)}, f32[32,24,128]{2,1,0:T(8,128)S(1)}, u32[]{:S(2)}, u32[]{:S(2)}) collective-permute-start(f32[32,24,128]{2,1,0:T(8,128)S(1)} %get-tuple-element.41), channel_id=1, source_target_pairs={{0,1},{1,0},{2,3},{3,2},{4,5},{5,4},{6,7},{7,6},{8,9},{9,8},{10,11... | collective-permute-start | bytes 1179656 | tf_op jit(solution)/shard_map/ppermute | solution.py:26
  69.3 1.7 %collective-permute-done.3 = f32[32,24,128]{2,1,0:T(8,128)S(1)} collective-permute-done((f32[32,24,128]{2,1,0:T(8,128)S(1)}, f32[32,24,128]{2,1,0:T(8,128)S(1)}, u32[]{:S(2)}, u32[]{:S(2)}) %collective-permute-start.3) | collective-permute-done | bytes 393248 | tf_op jit(solution)/shard_map/ppermute | solution.py:26
  71.0 0.1 add_convert_fusion
  71.0 22.3 %all_to_all.30 = bf16[32,24,128]{2,1,0:T(8,128)(2,1)S(1)} all-to-all(bf16[32,24,128]{2,1,0:T(8,128)(2,1)S(1)} %add_convert_fusion), channel_id=1, replica_groups={{0,16,32,48,64,80,96,112,128,144,160,176,192,208,224,240,256,272,288,30..., dimensions={0} | all-to-all | bytes 393216 | tf_op jit(solution)/shard_map/all_to_all | solution.py:42
  93.5 10.8 %all_to_all.31 = f32[8,10,128]{2,1,0:T(8,128)S(1)} all-to-all(f32[8,10,128]{2,1,0:T(8,128)S(1)} %pad_maximum_fusion.1), channel_id=1, replica_groups={{0,2,4,6,8,10,12,14},{1,3,5,7,9,11,13,15},{16,18,20,22,24,26,28,30},{17..., dimensions={0} | all-to-all | bytes 81920 | tf_op jit(solution)/shard_map/all_to_all | solution.py:42
  104.3 0.7 broadcast_in_dim.14
  104.9 4.8 %all-to-all-start.5 = ((f32[16,10,128]{2,1,0:T(8,128)}), f32[16,10,128]{2,1,0:T(8,128)S(1)}, u32[]{:S(2)}, u32[]{:S(2)}) async-start(f32[16,10,128]{2,1,0:T(8,128)} %broadcast_in_dim.14), calls=%async_computation.5 | async-start | bytes 262144 | tf_op jit(solution)/shard_map/all_to_all | solution.py:42
  109.7 0.2 shard_map.149
  109.9 0.7 reshape.99
  110.5 0.2 shard_map.150
  110.7 0.7 reshape.100
  111.4 5.6 %all-to-all-done.5.arrived = f32[16,10,128]{2,1,0:T(8,128)S(1)} async-done(((f32[16,10,128]{2,1,0:T(8,128)}), f32[16,10,128]{2,1,0:T(8,128)S(1)}, u32[]{:S(2)}, u32[]{:S(2)}) %all-to-all-start.5) | async-done | bytes 81952 | tf_op jit(solution)/shard_map/all_to_all | solution.py:42
  117.0 0.7 shard_map.148
  (12 shorter events, 0.2 us)
Async XLA Ops:
  0.6 39.8 %copy-start = (f32[69,4,128]{2,1,0:T(4,128)S(1)}, f32[69,4,128]{2,1,0:T(4,128)}, u32[]{:S(2)}) copy-start(f32[69,4,128]{2,1,0:T(4,128)} %param.10) | copy-start | bytes 423940
  0.6 0.8 copy-start.5
  2.1 13.4 %copy-start.3 = (bf16[4,128,128]{2,1,0:T(8,128)(2,1)S(1)}, bf16[4,128,128]{2,1,0:T(8,128)(2,1)}, u32[]{:S(2)}) copy-start(bf16[4,128,128]{2,1,0:T(8,128)(2,1)} %param.8) | copy-start | bytes 393220
  2.1 13.4 %copy-start.4 = (bf16[1,4,128,128]{3,2,1,0:T(8,128)(2,1)S(1)}, bf16[1,4,128,128]{3,2,1,0:T(8,128)(2,1)}, u32[]{:S(2)}) copy-start(bf16[1,4,128,128]{3,2,1,0:T(8,128)(2,1)} %param.9) | copy-start | bytes 393220
  2.1 24.1 %all-to-all-start = ((bf16[16,32,128]{2,1,0:T(8,128)(2,1)}), bf16[16,32,128]{2,1,0:T(8,128)(2,1)S(1)}, u32[]{:S(2)}, u32[]{:S(2)}) async-start(bf16[16,32,128]{2,1,0:T(8,128)(2,1)} %pad_maximum_fusion), calls=%async_computation | async-start | bytes 262144 | tf_op jit(solution)/shard_map/all_to_all | solution.py:42
  15.5 13.3 %copy-start.2 = (f32[49,128]{1,0:T(8,128)S(1)}, f32[49,128]{1,0:T(8,128)}, u32[]{:S(2)}) copy-start(f32[49,128]{1,0:T(8,128)} %taps.1) | copy-start | bytes 75268
  15.6 3.2 %collective-permute-start = (bf16[3,128,128]{2,1,0:T(8,128)(2,1)S(1)}, bf16[3,128,128]{2,1,0:T(8,128)(2,1)S(1)}, u32[]{:S(2)}, u32[]{:S(2)}) collective-permute-start(bf16[3,128,128]{2,1,0:T(8,128)(2,1)S(1)} %get-tuple-element.49), channel_id=1, source_target_pairs={{0,1},{1,0},{2,3},{3,2},{4,5},{5,4},{6,7},{7,6},{8,9},{9,8},{10,11... | collective-permute-start | bytes 294920 | tf_op jit(solution)/shard_map/ppermute | solution.py:26
  17.5 1.3 %collective-permute-start.1 = (bf16[3,128,128]{2,1,0:T(8,128)(2,1)S(1)}, bf16[3,128,128]{2,1,0:T(8,128)(2,1)S(1)}, u32[]{:S(2)}, u32[]{:S(2)}) collective-permute-start(bf16[3,128,128]{2,1,0:T(8,128)(2,1)S(1)} %get-tuple-element.48), channel_id=1, source_target_pairs={{1,2},{3,4},{5,6},{7,8},{9,10},{11,12},{13,14},{15,16},{17,18},{19... | collective-permute-start | bytes 294920 | tf_op jit(solution)/shard_map/ppermute | solution.py:32
  26.2 4.7 %collective-permute-start.2 = (bf16[16,32,128]{2,1,0:T(8,128)(2,1)S(1)}, bf16[16,32,128]{2,1,0:T(8,128)(2,1)S(1)}, u32[]{:S(2)}, u32[]{:S(2)}) collective-permute-start(bf16[16,32,128]{2,1,0:T(8,128)(2,1)S(1)} %all-to-all-done.mine), channel_id=1, source_target_pairs={{0,1},{1,0},{2,3},{3,2},{4,5},{5,4},{6,7},{7,6},{8,9},{9,8},{10,11... | collective-permute-start | bytes 393224 | tf_op jit(solution)/shard_map/ppermute | solution.py:26
  28.1 0.7 copy-start.6
  28.9 2.0 %copy-start.1 = (bf16[69,128]{1,0:T(8,128)(2,1)S(1)}, bf16[69,128]{1,0:T(8,128)(2,1)}, u32[]{:S(2)}) copy-start(bf16[69,128]{1,0:T(8,128)(2,1)} %readout.5) | copy-start | bytes 52996
  32.8 15.1 %all-to-all-start.1 = ((bf16[16,8,512]{2,1,0:T(8,128)(2,1)}), bf16[16,8,512]{2,1,0:T(8,128)(2,1)S(1)}, u32[]{:S(2)}, u32[]{:S(2)}) async-start(bf16[16,8,512]{2,1,0:T(8,128)(2,1)} %get-tuple-element.32), calls=%async_computation.1 | async-start | bytes 262144 | tf_op jit(solution)/shard_map/all_to_all | solution.py:42
  50.1 13.5 %all-to-all-start.2 = ((bf16[16,16,512]{2,1,0:T(8,128)(2,1)}), bf16[16,16,512]{2,1,0:T(8,128)(2,1)S(1)}, u32[]{:S(2)}, u32[]{:S(2)}) async-start(bf16[16,16,512]{2,1,0:T(8,128)(2,1)} %get-tuple-element.33), calls=%async_computation.2 | async-start | bytes 524288 | tf_op jit(solution)/shard_map/all_to_all | solution.py:42
  67.4 3.6 %collective-permute-start.3 = (f32[32,24,128]{2,1,0:T(8,128)S(1)}, f32[32,24,128]{2,1,0:T(8,128)S(1)}, u32[]{:S(2)}, u32[]{:S(2)}) collective-permute-start(f32[32,24,128]{2,1,0:T(8,128)S(1)} %get-tuple-element.41), channel_id=1, source_target_pairs={{0,1},{1,0},{2,3},{3,2},{4,5},{5,4},{6,7},{7,6},{8,9},{9,8},{10,11... | collective-permute-start | bytes 1179656 | tf_op jit(solution)/shard_map/ppermute | solution.py:26
  104.9 12.1 %all-to-all-start.5 = ((f32[16,10,128]{2,1,0:T(8,128)}), f32[16,10,128]{2,1,0:T(8,128)S(1)}, u32[]{:S(2)}, u32[]{:S(2)}) async-start(f32[16,10,128]{2,1,0:T(8,128)} %broadcast_in_dim.14), calls=%async_computation.5 | async-start | bytes 262144 | tf_op jit(solution)/shard_map/all_to_all | solution.py:42

commit v4 on v3

--- a/solution.py
+++ b/solution.py
@@ -169,24 +169,27 @@
     )
 
 
-def mlp_body(normed, mine, theirs, field, readout, gated, upper, residual, chunks):
-    points, channels = normed.shape
-    halves = [matrices(mine), matrices(theirs)]
-    wide = upper.shape[1] // 2
-    for k, (widen, _) in enumerate(halves):
-        upper[:, k * wide : (k + 1) * wide] = dot(normed[...], widen, (1, 1))
+def expand(normed, shards, gated, upper):
+    widen, shrink = matrices(shards)
+    upper[...] = dot(normed[...], widen, (1, 1))
 
     def step(i, carry):
         at = pl.ds(pl.multiple_of(i * 16, 16), 16)
         gated[at, :] = gelu_value(upper[at, :]).astype(BF16)
         return carry
 
-    lax.fori_loop(0, points // 16, step, 0, unroll=2)
-    mixed = sum(
-        dot(gated[:, k * wide : (k + 1) * wide], shrink, (1, 0))
-        for k, (_, shrink) in enumerate(halves)
-    )
-    residual[...] = (field[...].reshape(points, channels).astype(F32) + mixed).astype(BF16)
+    lax.fori_loop(0, upper.shape[0] // 16, step, 0, unroll=2)
+    return dot(gated[...], shrink, (1, 0))
+
+
+def first_body(normed, mine, gated, upper, mixed):
+    mixed[...] = expand(normed, mine, gated, upper)
+
+
+def second_body(normed, theirs, mixed, field, readout, gated, upper, residual, chunks):
+    points, channels = normed.shape
+    total = mixed[...] + expand(normed, theirs, gated, upper)
+    residual[...] = (field[...].reshape(points, channels).astype(F32) + total).astype(BF16)
     members = chunks.shape[0]
     spread = dot(selector(members * CHUNK_ROWS, readout.shape[0], 3, (0,), False), readout[...], (1, 0))
     outlook = dot(spread.astype(BF16), residual[...], (1, 1))
@@ -260,23 +263,25 @@
 
 
 def backward_body(
-    back, readout, residual, gated, slope, normed, scaled, inverse, gain, mine, theirs,
+    back, readout, residual, gated, other_gated, slope, other_slope, normed, scaled, inverse, gain, mine, theirs,
     widen_grad, shrink_grad, readout_grad, gain_grad, back_depth, gate, back_upper,
 ):
     members, height, points = back.shape
     halves = [matrices(mine), matrices(theirs)]
-    wide = slope.shape[1] // 2
+    wide = slope.shape[1]
     flow = back[...].reshape(members * height, points)
     spread = dot(selector(members * height, readout.shape[0], 4, (0,), False), readout[...], (1, 0))
     back_residual = dot(flow, spread.astype(BF16), (0, 0)).astype(BF16)
     for k, (_, shrink) in enumerate(halves):
         gate[:, k * wide : (k + 1) * wide] = dot(back_residual, shrink, (1, 1))
     readout_grad[...] = dot(flow, residual[...], (1, 0))
-    shrink_grad[...] = dot(gated[...], back_residual, (0, 0))
+    shrink_grad[:wide, :] = dot(gated[...], back_residual, (0, 0))
+    shrink_grad[wide:, :] = dot(other_gated[...], back_residual, (0, 0))
 
     def step(i, carry):
         at = pl.ds(pl.multiple_of(i * 16, 16), 16)
-        back_upper[at, :] = (gate[at, :] * slope[at, :]).astype(BF16)
+        back_upper[at, :wide] = (gate[at, :wide] * slope[at, :]).astype(BF16)
+        back_upper[at, wide:] = (gate[at, wide:] * other_slope[at, :]).astype(BF16)
         return carry
 
     lax.fori_loop(0, points // 16, step, 0, unroll=2)
@@ -336,13 +341,13 @@
 
 
 def gradient_body(
-    place, back, readout, residual, gated, slope, normed, scaled, inverse, gain, mine, theirs, loss,
+    place, back, readout, residual, gated, other_gated, slope, other_slope, normed, scaled, inverse, gain, mine, theirs, loss,
     field, partner, other, send, keep, ext, gate, back_upper, widen_grad, shrink_grad, readout_grad, gain_grad, back_depth, small,
 ):
     fill_rows(place, field, partner, other, ext)
     backward_body(
-        back, readout, residual, gated, slope, normed, scaled, inverse, gain, mine, theirs,
-        widen_grad, shrink_grad, readout_grad, gain_grad, back_depth, gate, back_upper,
+        back, readout, residual, gated, other_gated, slope, other_slope, normed, scaled, inverse,
+        gain, mine, theirs, widen_grad, shrink_grad, readout_grad, gain_grad, back_depth, gate, back_upper,
     )
     pack_body(
         back_depth, ext, widen_grad, shrink_grad, readout_grad, gain_grad, loss,
@@ -393,7 +398,6 @@
         axis=1,
     )
     mine = exchange(pair, AXES, weight_groups(members, bands))
-    mine, partner, other = lax.optimization_barrier((mine, partner, other))
     theirs = core_swap(mine)
     latitude = (band * rows + jnp.arange(points, dtype=jnp.int32) // zonal).astype(F32)
     area = jnp.cos(math.pi * ((latitude + 0.5) / latitudes - 0.5))
@@ -411,18 +415,28 @@
         scalars=1,
         vectors=5,
     )(place, field, partner, other, stencil_taps, gain)
-    gated, upper, residual, chunks = vmem_call(
-        mlp_body,
+    gated, upper, mixed = vmem_call(
+        first_body,
+        [((points, hidden // 2), BF16), ((points, hidden // 2), F32), ((points, channels), F32)],
+        vectors=2,
+    )(normed, mine)
+    other_gated, other_upper, residual, chunks = vmem_call(
+        second_body,
         [
-            ((points, hidden), BF16),
-            ((points, hidden), F32),
+            ((points, hidden // 2), BF16),
+            ((points, hidden // 2), F32),
             ((points, channels), BF16),
             ((members, CHUNK_ROWS, points), BF16),
         ],
         vectors=5,
-    )(normed, mine, theirs, field, readout_matrix)
+    )(normed, theirs, mixed, field, readout_matrix)
     everyone = exchange(chunks, "ens")
-    (slope,) = vmem_call(slope_body, [((points, hidden), F32)], vectors=1, aliases={0: 0})(upper)
+    slope, other_slope = (
+        vmem_call(
+            slope_body, [((points, hidden // 2), F32)], vectors=1, aliases={0: 0}
+        )(half_upper)[0]
+        for half_upper in (upper, other_upper)
+    )
     first = jnp.minimum(member * PER_CHUNK, variables - PER_CHUNK)
     truth = lax.dynamic_slice_in_dim(observed_truth, first, PER_CHUNK, axis=0)
     (outlook,) = vmem_call(outlook_body, [((variables, points), BF16)], vectors=2)(
@@ -456,10 +470,10 @@
             pltpu.VMEM((members * share, channels), F32),
         ],
         scalars=1,
-        vectors=15,
+        vectors=17,
     )(
-        place, back, readout_matrix, residual, gated, slope, normed, scaled, inverse, gain, mine,
-        theirs, loss, field, partner, other,
+        place, back, readout_matrix, residual, gated, other_gated, slope, other_slope, normed,
+        scaled, inverse, gain, mine, theirs, loss, field, partner, other,
     )
 
     total = (keep + core_swap(send)).astype(BF16)

time: 118 us -> 125 us (1.059)
  starting transfers between devices: 36.6 us -> 39.1 us
  blocking collectives: 33.1 us -> 34.9 us
    ppermute x3, starting transfers between devices: 5.75 us -> 8.26 us  [core_swap(): return lax.ppermute(value, 'lat', [(i, i ^ 1) for i in range(count)])]
    all_to_all x4, waiting for transfers between devices: 28.7 us -> 30.6 us  [exchange(): lax.all_to_all(value, axis, 0, 0, tiled=True, axis_index_groups=groups)]
    all_to_all x2, blocking collectives: 33.1 us -> 34.9 us  [exchange(): lax.all_to_all(value, axis, 0, 0, tiled=True, axis_index_groups=groups)]
    pallas_call x8 -> x10, Pallas kernels: 11.6 us -> 12.8 us  [run(): return call(*operands)]
  transfers between devices with their start and end apart: 8 -> 8, of which waited for: 6 -> 5; matrix products, arithmetic and copies ran while one was open for 1% -> 1% of each run, Pallas kernels for 3% -> 4%
where the time goes in v4:
time: 125 us; the launch traced here: 124 us
  starting transfers between devices  39.1 us (31%)
  blocking collectives  34.9 us (28%)
  waiting for transfers between devices  32 us (26%)
  Pallas kernels  12.8 us (10%)
  local copies, waits for them, and re-layouts  3.53 us (3%)
    all_to_all x2, blocking collectives, exchange(): lax.all_to_all(value, axis, 0, 0, tiled=True, axis_index_groups=groups)  34.9 us
    all_to_all x4, waiting for transfers between devices, exchange(): lax.all_to_all(value, axis, 0, 0, tiled=True, axis_index_groups=groups)  30.6 us
    all_to_all x4, starting transfers between devices, exchange(): lax.all_to_all(value, axis, 0, 0, tiled=True, axis_index_groups=groups)  30.1 us
    pallas_call x10, Pallas kernels, run(): return call(*operands)  12.8 us
    ppermute x3, starting transfers between devices, core_swap(): return lax.ppermute(value, 'lat', [(i, i ^ 1) for i in range(count)])  8.26 us
  transfers between devices with their start and end apart: 8, of which 5 were waited for; matrix products, arithmetic and copies ran while one was open for 1% of the time, Pallas kernels for 4%

profile of v4, /device:TPU:8, one launch (start us, length us, event | category | flops | bytes accessed | tf_op | source)
XLA Modules:
  0.0 124.1 jit_solution(16852820785520771967)
XLA Ops:
  0.6 0.0 copy-start
  0.6 0.0 copy-start.5
  0.7 0.7 broadcast_in_dim.11
  1.4 0.0 copy-done.5
  1.4 0.7 pad_maximum_fusion
  2.1 0.0 copy-start.3
  2.1 0.0 copy-start.4
  2.1 13.3 %all-to-all-start = ((bf16[16,32,128]{2,1,0:T(8,128)(2,1)}), bf16[16,32,128]{2,1,0:T(8,128)(2,1)S(1)}, u32[]{:S(2)}, u32[]{:S(2)}) async-start(bf16[16,32,128]{2,1,0:T(8,128)(2,1)} %pad_maximum_fusion), calls=%async_computation | async-start | bytes 262144 | tf_op jit(solution)/shard_map/all_to_all | solution.py:42
  15.5 0.0 copy-done.3
  15.5 0.0 copy-done.4
  15.5 10.7 %all-to-all-done.mine = bf16[16,32,128]{2,1,0:T(8,128)(2,1)S(1)} async-done(((bf16[16,32,128]{2,1,0:T(8,128)(2,1)}), bf16[16,32,128]{2,1,0:T(8,128)(2,1)S(1)}, u32[]{:S(2)}, u32[]{:S(2)}) %all-to-all-start) | async-done | bytes 131104 | tf_op jit(solution)/shard_map/all_to_all | solution.py:42
  26.2 1.9 %collective-permute-start.2 = (bf16[16,32,128]{2,1,0:T(8,128)(2,1)S(1)}, bf16[16,32,128]{2,1,0:T(8,128)(2,1)S(1)}, u32[]{:S(2)}, u32[]{:S(2)}) collective-permute-start(bf16[16,32,128]{2,1,0:T(8,128)(2,1)S(1)} %all-to-all-done.mine), channel_id=1, source_target_pairs={{0,1},{1,0},{2,3},{3,2},{4,5},{5,4},{6,7},{7,6},{8,9},{9,8},{10,11... | collective-permute-start | bytes 393224 | tf_op jit(solution)/shard_map/ppermute | solution.py:26
  28.1 0.0 copy-start.2
  28.2 2.4 %collective-permute-start = (bf16[3,128,128]{2,1,0:T(8,128)(2,1)S(1)}, bf16[3,128,128]{2,1,0:T(8,128)(2,1)S(1)}, u32[]{:S(2)}, u32[]{:S(2)}) collective-permute-start(bf16[3,128,128]{2,1,0:T(8,128)(2,1)S(1)} %get-tuple-element.49), channel_id=1, source_target_pairs={{0,1},{1,0},{2,3},{3,2},{4,5},{5,4},{6,7},{7,6},{8,9},{9,8},{10,11... | collective-permute-start | bytes 294920 | tf_op jit(solution)/shard_map/ppermute | solution.py:26
  30.6 0.7 collective-permute-start.1
  31.2 0.0 copy-start.6
  31.3 0.6 copy-done.6
  31.9 0.1 pad_add_fusion.place
  32.0 0.0 collective-permute-done.partner
  32.0 0.0 collective-permute-done.1.other
  32.0 0.0 copy-done.2
  32.0 2.0 %shard_map.143 = (f32[512,128]{1,0:T(8,128)S(1)}, f32[512,128]{1,0:T(8,128)S(1)}, bf16[512,128]{1,0:T(8,128)(2,1)S(1)}) custom-call(s32[2]{0:T(128)S(1)} %pad_add_fusion.place, bf16[4,128,128]{2,1,0:T(8,128)(2,1)S(1)} %fusion.field, bf16[3,128,128]{2,1,0:T(8,128)(2,1)S(1)} %collective-permute-done.partner, ...), custom_call_target="tpu_custom_call" | custom-call | tf_op jit(solution)/shard_map/pallas_call | solution.py:101
  34.0 0.0 copy-start.1
  34.0 0.9 shard_map.144
  34.9 0.0 collective-permute-done.2.theirs
  34.9 0.0 copy-done.1
  34.9 1.7 %shard_map.145 = (bf16[512,256]{1,0:T(8,128)(2,1)S(1)}, f32[512,256]{1,0:T(8,128)S(1)}, bf16[512,128]{1,0:T(8,128)(2,1)S(1)}, bf16[16,8,512]{2,1,0:T(8,128)(2,1)}) custom-call(bf16[512,128]{1,0:T(8,128)(2,1)S(1)} %get-tuple-element.28.normed, bf16[16,32,128]{2,1,0:T(8,128)(2,1)S(1)} %collective-permute-done.2.theirs, ...), custom_call_target="tpu_custom_call" | custom-call | tf_op jit(solution)/shard_map/pallas_call | solution.py:101
  36.7 7.5 %all-to-all-start.1 = ((bf16[16,8,512]{2,1,0:T(8,128)(2,1)}), bf16[16,8,512]{2,1,0:T(8,128)(2,1)S(1)}, u32[]{:S(2)}, u32[]{:S(2)}) async-start(bf16[16,8,512]{2,1,0:T(8,128)(2,1)} %get-tuple-element.30), calls=%async_computation.1 | async-start | bytes 262144 | tf_op jit(solution)/shard_map/all_to_all | solution.py:42
  44.2 0.1 fusion.8.weight
  44.2 0.0 copy-done
  44.3 7.2 %all-to-all-done.1.everyone = bf16[16,8,512]{2,1,0:T(8,128)(2,1)S(1)} async-done(((bf16[16,8,512]{2,1,0:T(8,128)(2,1)}), bf16[16,8,512]{2,1,0:T(8,128)(2,1)S(1)}, u32[]{:S(2)}, u32[]{:S(2)}) %all-to-all-start.1) | async-done | bytes 131104 | tf_op jit(solution)/shard_map/all_to_all | solution.py:42
  51.4 2.2 %shard_map.146 = (bf16[16,16,512]{2,1,0:T(8,128)(2,1)}, f32[1,128]{1,0:T(1,128)S(1)}) custom-call(s32[2]{0:T(128)S(1)} %pad_add_fusion.place, bf16[16,8,512]{2,1,0:T(8,128)(2,1)S(1)} %all-to-all-done.1.everyone, f32[5,4,128]{2,1,0:T(4,128)S(1)} %constant_dynamic-slice_fusion.truth, f32[1,512]{1,0:T(1,128)S(1)} %fusion.8.weight), custom_call_target="tpu_custom_call" | custom-call | tf_op jit(solution)/shard_map/pallas_call | solution.py:101
  53.6 4.5 %all-to-all-start.2 = ((bf16[16,16,512]{2,1,0:T(8,128)(2,1)}), bf16[16,16,512]{2,1,0:T(8,128)(2,1)S(1)}, u32[]{:S(2)}, u32[]{:S(2)}) async-start(bf16[16,16,512]{2,1,0:T(8,128)(2,1)} %get-tuple-element.31), calls=%async_computation.2 | async-start | bytes 524288 | tf_op jit(solution)/shard_map/all_to_all | solution.py:42
  58.1 0.6 shard_map.147.slope
  58.8 0.6 shard_map.148.other_slope
  59.4 7.2 %all-to-all-done.2.back = bf16[16,16,512]{2,1,0:T(8,128)(2,1)S(1)} async-done(((bf16[16,16,512]{2,1,0:T(8,128)(2,1)}), bf16[16,16,512]{2,1,0:T(8,128)(2,1)S(1)}, u32[]{:S(2)}, u32[]{:S(2)}) %all-to-all-start.2) | async-done | bytes 262176 | tf_op jit(solution)/shard_map/all_to_all | solution.py:42
  66.6 3.7 %shard_map.149 = (f32[32,24,128]{2,1,0:T(8,128)S(1)}, f32[32,24,128]{2,1,0:T(8,128)S(1)}) custom-call(s32[2]{0:T(128)S(1)} %pad_add_fusion.place, bf16[16,16,512]{2,1,0:T(8,128)(2,1)S(1)} %all-to-all-done.2.back, bf16[69,128]{1,0:T(8,128)(2,1)S(1)} %copy-done.1, bf16[512,128]{1,0:T(8,128)(2,1)S(1)} %get-tuple-element.32.residual, ...), custom_call_target="tpu_custom_call" | custom-call | tf_op jit(solution)/shard_map/pallas_call | solution.py:101
  70.3 3.9 %collective-permute-start.3 = (f32[32,24,128]{2,1,0:T(8,128)S(1)}, f32[32,24,128]{2,1,0:T(8,128)S(1)}, u32[]{:S(2)}, u32[]{:S(2)}) collective-permute-start(f32[32,24,128]{2,1,0:T(8,128)S(1)} %get-tuple-element.41), channel_id=1, source_target_pairs={{0,1},{1,0},{2,3},{3,2},{4,5},{5,4},{6,7},{7,6},{8,9},{9,8},{10,11... | collective-permute-start | bytes 1179656 | tf_op jit(solution)/shard_map/ppermute | solution.py:26
  74.3 1.3 %collective-permute-done.3 = f32[32,24,128]{2,1,0:T(8,128)S(1)} collective-permute-done((f32[32,24,128]{2,1,0:T(8,128)S(1)}, f32[32,24,128]{2,1,0:T(8,128)S(1)}, u32[]{:S(2)}, u32[]{:S(2)}) %collective-permute-start.3) | collective-permute-done | bytes 393248 | tf_op jit(solution)/shard_map/ppermute | solution.py:26
  75.6 24.2 %all_to_all.30 = bf16[32,24,128]{2,1,0:T(8,128)(2,1)S(1)} all-to-all(bf16[32,24,128]{2,1,0:T(8,128)(2,1)S(1)} %add_convert_fusion), channel_id=1, replica_groups={{0,16,32,48,64,80,96,112,128,144,160,176,192,208,224,240,256,272,288,30..., dimensions={0} | all-to-all | bytes 393216 | tf_op jit(solution)/shard_map/all_to_all | solution.py:42
  99.9 10.8 %all_to_all.31 = f32[8,10,128]{2,1,0:T(8,128)S(1)} all-to-all(f32[8,10,128]{2,1,0:T(8,128)S(1)} %pad_maximum_fusion.1), channel_id=1, replica_groups={{0,2,4,6,8,10,12,14},{1,3,5,7,9,11,13,15},{16,18,20,22,24,26,28,30},{17..., dimensions={0} | all-to-all | bytes 81920 | tf_op jit(solution)/shard_map/all_to_all | solution.py:42
  110.7 0.7 broadcast_in_dim.14
  111.3 4.8 %all-to-all-start.5 = ((f32[16,10,128]{2,1,0:T(8,128)}), f32[16,10,128]{2,1,0:T(8,128)S(1)}, u32[]{:S(2)}, u32[]{:S(2)}) async-start(f32[16,10,128]{2,1,0:T(8,128)} %broadcast_in_dim.14), calls=%async_computation.5 | async-start | bytes 262144 | tf_op jit(solution)/shard_map/all_to_all | solution.py:42
  116.1 0.2 shard_map.151
  116.3 0.7 reshape.99
  117.0 0.2 shard_map.152
  117.1 0.7 reshape.100
  117.8 5.6 %all-to-all-done.5.arrived = f32[16,10,128]{2,1,0:T(8,128)S(1)} async-done(((f32[16,10,128]{2,1,0:T(8,128)}), f32[16,10,128]{2,1,0:T(8,128)S(1)}, u32[]{:S(2)}, u32[]{:S(2)}) %all-to-all-start.5) | async-done | bytes 81952 | tf_op jit(solution)/shard_map/all_to_all | solution.py:42
  123.5 0.7 shard_map.150
  (13 shorter events, 0.2 us)
Async XLA Ops:
  0.6 43.6 %copy-start = (f32[69,4,128]{2,1,0:T(4,128)S(1)}, f32[69,4,128]{2,1,0:T(4,128)}, u32[]{:S(2)}) copy-start(f32[69,4,128]{2,1,0:T(4,128)} %param.10) | copy-start | bytes 423940
  0.6 0.8 copy-start.5
  2.1 13.4 %copy-start.3 = (bf16[4,128,128]{2,1,0:T(8,128)(2,1)S(1)}, bf16[4,128,128]{2,1,0:T(8,128)(2,1)}, u32[]{:S(2)}) copy-start(bf16[4,128,128]{2,1,0:T(8,128)(2,1)} %param.8) | copy-start | bytes 393220
  2.1 13.4 %copy-start.4 = (bf16[1,4,128,128]{3,2,1,0:T(8,128)(2,1)S(1)}, bf16[1,4,128,128]{3,2,1,0:T(8,128)(2,1)}, u32[]{:S(2)}) copy-start(bf16[1,4,128,128]{3,2,1,0:T(8,128)(2,1)} %param.9) | copy-start | bytes 393220
  2.1 24.1 %all-to-all-start = ((bf16[16,32,128]{2,1,0:T(8,128)(2,1)}), bf16[16,32,128]{2,1,0:T(8,128)(2,1)S(1)}, u32[]{:S(2)}, u32[]{:S(2)}) async-start(bf16[16,32,128]{2,1,0:T(8,128)(2,1)} %pad_maximum_fusion), calls=%async_computation | async-start | bytes 262144 | tf_op jit(solution)/shard_map/all_to_all | solution.py:42
  26.2 8.7 %collective-permute-start.2 = (bf16[16,32,128]{2,1,0:T(8,128)(2,1)S(1)}, bf16[16,32,128]{2,1,0:T(8,128)(2,1)S(1)}, u32[]{:S(2)}, u32[]{:S(2)}) collective-permute-start(bf16[16,32,128]{2,1,0:T(8,128)(2,1)S(1)} %all-to-all-done.mine), channel_id=1, source_target_pairs={{0,1},{1,0},{2,3},{3,2},{4,5},{5,4},{6,7},{7,6},{8,9},{9,8},{10,11... | collective-permute-start | bytes 393224 | tf_op jit(solution)/shard_map/ppermute | solution.py:26
  28.1 3.9 %copy-start.2 = (f32[49,128]{1,0:T(8,128)S(1)}, f32[49,128]{1,0:T(8,128)}, u32[]{:S(2)}) copy-start(f32[49,128]{1,0:T(8,128)} %taps.1) | copy-start | bytes 75268
  28.2 3.8 %collective-permute-start = (bf16[3,128,128]{2,1,0:T(8,128)(2,1)S(1)}, bf16[3,128,128]{2,1,0:T(8,128)(2,1)S(1)}, u32[]{:S(2)}, u32[]{:S(2)}) collective-permute-start(bf16[3,128,128]{2,1,0:T(8,128)(2,1)S(1)} %get-tuple-element.49), channel_id=1, source_target_pairs={{0,1},{1,0},{2,3},{3,2},{4,5},{5,4},{6,7},{7,6},{8,9},{9,8},{10,11... | collective-permute-start | bytes 294920 | tf_op jit(solution)/shard_map/ppermute | solution.py:26
  30.6 1.4 %collective-permute-start.1 = (bf16[3,128,128]{2,1,0:T(8,128)(2,1)S(1)}, bf16[3,128,128]{2,1,0:T(8,128)(2,1)S(1)}, u32[]{:S(2)}, u32[]{:S(2)}) collective-permute-start(bf16[3,128,128]{2,1,0:T(8,128)(2,1)S(1)} %get-tuple-element.48), channel_id=1, source_target_pairs={{1,2},{3,4},{5,6},{7,8},{9,10},{11,12},{13,14},{15,16},{17,18},{19... | collective-permute-start | bytes 294920 | tf_op jit(solution)/shard_map/ppermute | solution.py:32
  31.2 0.7 copy-start.6
  34.0 0.9 copy-start.1
  36.7 14.8 %all-to-all-start.1 = ((bf16[16,8,512]{2,1,0:T(8,128)(2,1)}), bf16[16,8,512]{2,1,0:T(8,128)(2,1)S(1)}, u32[]{:S(2)}, u32[]{:S(2)}) async-start(bf16[16,8,512]{2,1,0:T(8,128)(2,1)} %get-tuple-element.30), calls=%async_computation.1 | async-start | bytes 262144 | tf_op jit(solution)/shard_map/all_to_all | solution.py:42
  53.6 13.0 %all-to-all-start.2 = ((bf16[16,16,512]{2,1,0:T(8,128)(2,1)}), bf16[16,16,512]{2,1,0:T(8,128)(2,1)S(1)}, u32[]{:S(2)}, u32[]{:S(2)}) async-start(bf16[16,16,512]{2,1,0:T(8,128)(2,1)} %get-tuple-element.31), calls=%async_computation.2 | async-start | bytes 524288 | tf_op jit(solution)/shard_map/all_to_all | solution.py:42
  70.3 5.3 %collective-permute-start.3 = (f32[32,24,128]{2,1,0:T(8,128)S(1)}, f32[32,24,128]{2,1,0:T(8,128)S(1)}, u32[]{:S(2)}, u32[]{:S(2)}) collective-permute-start(f32[32,24,128]{2,1,0:T(8,128)S(1)} %get-tuple-element.41), channel_id=1, source_target_pairs={{0,1},{1,0},{2,3},{3,2},{4,5},{5,4},{6,7},{7,6},{8,9},{9,8},{10,11... | collective-permute-start | bytes 1179656 | tf_op jit(solution)/shard_map/ppermute | solution.py:26
  111.3 12.1 %all-to-all-start.5 = ((f32[16,10,128]{2,1,0:T(8,128)}), f32[16,10,128]{2,1,0:T(8,128)S(1)}, u32[]{:S(2)}, u32[]{:S(2)}) async-start(f32[16,10,128]{2,1,0:T(8,128)} %broadcast_in_dim.14), calls=%async_computation.5 | async-start | bytes 262144 | tf_op jit(solution)/shard_map/all_to_all | solution.py:42
